TPU v7x, 32 devices: a whole 2x2x4 slice. The times are simulated.
32 devices in a mesh: img: 2 (over y), sub: 4 (over z), rng: 4 (over x, core).
Axes of the slice: x: 2, y: 2, z: 4, core: 2. Of those that a mesh axis runs over, the one named last changes fastest.
Arguments:
- image: bfloat16 [2, 16, 128, 4096], P(None, ('img', 'sub'), None, 'rng'), parts along dimension 1, may hold values from -6 to 6
- interp_weights: bfloat16 [4, 2, 2, 2, 128, 128], replicated, may hold values from -0.25 to 0.25
- range_taps: float32 [4, 4], replicated, may hold values from -2 to 2
- range_shifts: int32 [4, 2, 128], replicated, may hold values from -8 to 5
Outputs:
- merged_image: bfloat16 [2, 16, 128, 4096], P(None, ('img', 'sub'), None, 'rng'), parts along dimension 1
There are 2 independent parts, one for each index of `img`. A program takes and returns all parts, laid end to end along the dimension named above; an argument that names none is the same for every part. Nothing has to cross between parts.
All inputs are finite; a program needn't handle non-finite values.
Results may differ from a plain program's by a relative error of at most 0.0095.
Values may be sent and summed in bfloat16 or wider, within the bound.
No kernel may reach another device: no remote copies, remote signals or barrier semaphores. Data moves between devices by JAX's collectives and lax.ppermute only.
A program may use at most 64 MiB of HBM per device.

v0:
```python
import math

import jax
import jax.numpy as jnp
from jax import lax
from jax.sharding import PartitionSpec as P

ANGLES = 128
RANGE = 4096
RIM = 8
TAPS = 4
LEVELS = 4


phase_step = 2.0 * math.pi / 64.0


def padded_2(cells, sides, width):
    for axis, dim in sides:
        count = lax.axis_size(axis)
        ends = count - 1
        head = lax.slice_in_dim(cells, 0, width, axis=dim)
        tail = lax.slice_in_dim(cells, cells.shape[dim] - width, cells.shape[dim], axis=dim)
        cells = jnp.concatenate(
            [
                lax.ppermute(tail, axis, [(i, (i + 1) % count) for i in range(ends)]),
                cells,
                lax.ppermute(head, axis, [((i + 1) % count, i) for i in range(ends)]),
            ],
            axis=dim,
        )
    return cells


def from_partner(value, axis, stride):
    mask = 2**stride
    pairs = [(source, source ^ mask) for source in range(lax.axis_size(axis))]
    return lax.ppermute(value, axis, pairs)


def rotate(merged_sum, level_index, half_index, range_start, range_width):
    angle_rows = half_index * ANGLES + jnp.arange(ANGLES, dtype=jnp.int32)
    range_cols = range_start + jnp.arange(range_width, dtype=jnp.int32)
    wrapped = range_cols[None, :] * (angle_rows[:, None] + 1) * (7 + level_index) % 64
    phase = wrapped.astype(jnp.float32) * phase_step
    cosine = jnp.cos(phase)
    sinus = jnp.sin(phase)
    return jnp.stack(
        [
            merged_sum[0] * cosine - merged_sum[1] * sinus,
            merged_sum[0] * sinus + merged_sum[1] * cosine,
        ]
    )


def level_coef(range_taps, range_shifts, level_index, side_index):
    offsets = jnp.arange(2 * RIM + 1, dtype=jnp.int32) - RIM
    tap_ids = jnp.arange(TAPS, dtype=jnp.int32)
    hits = (
        range_shifts[level_index, side_index][:, None, None] + tap_ids[None, :, None]
        == offsets[None, None, :]
    )
    return jnp.einsum(
        "t,ato->ao",
        range_taps[level_index],
        hits.astype(jnp.float32),
        precision=lax.Precision.HIGHEST,
    )


def interpolate(padded, coef, range_width):
    total = None
    for offset_index in range(2 * RIM + 1):
        term = coef[:, offset_index, None] * padded[
            ..., offset_index : offset_index + range_width
        ].astype(jnp.float32)
        total = term if total is None else total + term
    return total.astype(jnp.bfloat16)


def block_of(weight_pair):
    return jnp.stack(
        [jnp.stack([weight_pair[0], -weight_pair[1]]), jnp.stack([weight_pair[1], weight_pair[0]])]
    )


def combine_sides(lower_rows, upper_rows, weights_level, half_index):
    chosen = lax.dynamic_index_in_dim(weights_level, half_index, 1, keepdims=False)
    merged_sum = None
    for side_index, source in ((0, lower_rows), (1, upper_rows)):
        product = jnp.einsum(
            "xcij,cgjr->xgir",
            block_of(chosen[side_index]),
            source,
            preferred_element_type=jnp.float32,
        )
        merged_sum = product if merged_sum is None else merged_sum + product
    return merged_sum


def on_device(image, interp_weights, range_taps, range_shifts):
    range_width = image.shape[3]
    sub_count = lax.axis_size("sub")
    bit_count = sub_count.bit_length() - 1
    sub_index = lax.axis_index("sub")
    range_start = lax.axis_index("rng") * range_width
    current = padded_2(image, (("rng", 3),), LEVELS * RIM)
    margin = LEVELS * RIM
    for level_index in range(LEVELS):
        bit = level_index % bit_count
        own_half = sub_index // 2**bit % 2
        padded = current
        margin = margin - RIM
        out_width = range_width + 2 * margin
        coef = jnp.where(
            own_half == 0,
            level_coef(range_taps, range_shifts, level_index, 0),
            level_coef(range_taps, range_shifts, level_index, 1),
        )
        own_rows = interpolate(padded, coef, out_width)
        partner = from_partner(own_rows, "sub", bit)
        lower_rows = jnp.where(own_half == 0, own_rows, partner)
        upper_rows = jnp.where(own_half == 0, partner, own_rows)
        merged = combine_sides(lower_rows, upper_rows, interp_weights[level_index], own_half)
        turned = rotate(merged, level_index, own_half, range_start - margin, out_width)
        global_cols = range_start - margin + jnp.arange(out_width, dtype=jnp.int32)
        inside = jnp.logical_and(global_cols >= 0, global_cols < RANGE)
        turned = jnp.where(inside, turned, 0.0)
        current = turned.astype(jnp.bfloat16)
    return current


def solution(mesh):
    return jax.shard_map(
        on_device,
        mesh=mesh,
        in_specs=(P(None, ("img", "sub"), None, "rng"), P(), P(), P()),
        out_specs=P(None, ("img", "sub"), None, "rng"),
        check_vma=False,
    )
```

profile of v0, /device:TPU:0, one launch (start us, length us, event | category | flops | bytes accessed | tf_op | source)
XLA Modules:
  0.0 204.4 jit_solution(337052777099542682)
XLA Ops:
  0.0 1.7 copy.8
  1.7 1.3 collective-permute-start.1
  3.0 3.0 %collective-permute-start = (bf16[2,2,128,32]{2,3,1,0:T(8,128)(2,1)S(1)}, bf16[2,2,128,32]{2,3,1,0:T(8,128)(2,1)S(1)}, u32[]{:S(2)}, u32[]{:S(2)}) collective-permute-start(bf16[2,2,128,32]{2,3,1,0:T(8,128)(2,1)S(1)} %get-tuple-element.49), channel_id=1, source_target_pairs={{0,1},{1,2},{2,3},{4,5},{5,6},{6,7},{8,9},{9,10},{10,11},{12,13},{... | collective-permute-start | bytes 98312 | tf_op jit(solution)/shard_map/ppermute | solution.py:26
  6.1 0.1 fusion.84
  6.4 0.7 iota_add_fusion.8
  7.0 0.6 compare_and_fusion
  7.6 0.6 iota_add_fusion.9
  8.2 0.6 compare_and_fusion.1
  8.8 0.1 iota_add_fusion.6
  8.9 0.1 iota_add_fusion.4
  9.0 0.1 iota_add_fusion.2
  9.1 0.1 iota_add_fusion
  9.3 2.5 %select_reduce_fusion.6 = (f32[128,17]{1,0:T(8,128)}, f32[128,17]{1,0:T(8,128)}, f32[128,17]{1,0:T(8,128)}, f32[128,17]{1,0:T(8,128)}, f32[128,17]{1,0:T(8,128)}...) fusion(f32[4]{0:T(128)S(1)} %get-tuple-element.169, s32[128,4]{1,0:T(8,128)S(1)} %get-tuple-element.177, ...), kind=kLoop, calls=%fused_computation.96 | loop fusion | flops 191488 | bytes 86148
  11.9 0.6 slice_bitcast_fusion.64
  12.6 0.6 iota_add_fusion.10
  13.2 0.7 dynamic-slice_bitcast_fusion.1
  13.9 0.7 maximum_bitcast_fusion.18
  14.5 0.7 maximum_bitcast_fusion.16
  15.2 0.7 maximum_bitcast_fusion.22
  15.8 0.7 maximum_bitcast_fusion.20
  16.5 0.6 compare_and_fusion.2
  17.3 0.4 copy-done.42
  17.9 4.7 %add_convert_fusion = bf16[2,2,128,1072]{2,3,1,0:T(8,128)(2,1)S(1)} fusion(bf16[2,2,128,1088]{2,3,1,0:T(8,128)(2,1)S(1)} %pad_maximum_fusion, f32[128]{0:T(128)S(1)} %get-tuple-element.135, f32[128]{0:T(128)S(1)} %get-tuple-element.136, f32[128]{0:T(128)S(1)} %get-tuple-element.137, f32[128]{0:T(128)S(1)} %get-tuple-element.138, ...), kind=kLoop, calls=%fused_computation.14 | loop fusion | flops 27992064 | bytes 19767808 | tf_op jit(solution)/shard_map/convert_element_type | solution.py:78
  22.7 3.1 %collective-permute-start.2 = (bf16[2,2,128,1072]{2,3,1,0:T(8,128)(2,1)S(1)}, bf16[2,2,128,1072]{2,3,1,0:T(8,128)(2,1)S(1)}, u32[]{:S(2)}, u32[]{:S(2)}) collective-permute-start(bf16[2,2,128,1072]{2,3,1,0:T(8,128)(2,1)S(1)} %add_convert_fusion), channel_id=1, source_target_pairs={{0,4},{4,0},{8,12},{12,8},{1,5},{5,1},{9,13},{13,9},{2,6},{6,2},{1... | collective-permute-start | bytes 3293192 | tf_op jit(solution)/shard_map/ppermute | solution.py:38
  26.0 1.5 fusion.76
  27.6 2.2 %fusion.45 = (f32[128,1072]{0,1:T(8,128)S(1)}, f32[128,1072]{0,1:T(8,128)S(1)}) fusion(s32[128]{0:T(128)S(1)} %add_add_fusion.1, s32[1072]{0:T(1024)S(1)} %copy-done.30), kind=kLoop, calls=%fused_computation.83 | loop fusion | flops 2058240 | bytes 1102528 | tf_op jit(solution)/shard_map/cos | solution.py:46
  29.8 20.5 %collective-permute-done.2 = bf16[2,2,128,1072]{2,3,1,0:T(8,128)(2,1)S(1)} collective-permute-done((bf16[2,2,128,1072]{2,3,1,0:T(8,128)(2,1)S(1)}, bf16[2,2,128,1072]{2,3,1,0:T(8,128)(2,1)S(1)}, u32[]{:S(2)}, u32[]{:S(2)}) %collective-permute-start.2) | collective-permute-done | bytes 1097760 | tf_op jit(solution)/shard_map/ppermute | solution.py:38
  50.4 5.8 %select_bitcast_fusion.1 = (bf16[2,2,128,1072,1]{2,3,1,0,4:T(8,128)(2,1)S(1)}, bf16[2,2,128,1072,1]{2,3,1,0,4:T(8,128)(2,1)S(1)}) fusion(bf16[2,2,128,1072]{2,3,1,0:T(8,128)(2,1)S(1)} %collective-permute-done.2, pred[]{:T(512)S(6)} %eq.70, bf16[2,2,128,1088]{2,3,1,0:T(8,128)(2,1)S(1)} %pad_maximum_fusion, f32[128]{0:T(128)} %copy-done.35, f32[128]{0:T(128)} %copy-done.36, ...), kind=kLoop, calls=%fused_computation.32 | loop fusion | flops 29089792 | bytes 21963264 | tf_op jit(solution)/shard_map/jit(_where)/select_n | solution.py:122
  56.3 0.5 convolution_bitcast_fusion.4
  56.8 0.3 copy-done.7
  57.1 0.5 fusion.3
  57.6 0.3 multiply_subtract_fusion
  57.9 0.4 copy-done.33
  58.3 0.3 fusion.6
  58.7 4.8 %add_convert_fusion.1 = bf16[2,2,128,1056]{2,3,0,1:T(8,128)(2,1)S(1)} fusion(bf16[2,2,128,1072]{2,3,0,1:T(8,128)(2,1)S(1)} %fusion.6, f32[128]{0:T(128)S(1)} %get-tuple-element.118, f32[128]{0:T(128)S(1)} %get-tuple-element.119, f32[128]{0:T(128)S(1)} %get-tuple-element.120, f32[128]{0:T(128)S(1)} %get-tuple-element.121, f32[128]{0:T(128)S(1)} %get-tuple-element.122, ...), kind=kLoop, calls=%fused_computation.17 | loop fusion | flops 27574272 | bytes 19472896 | tf_op jit(solution)/shard_map/convert_element_type | solution.py:78
  63.5 3.5 %collective-permute-start.3 = (bf16[2,2,128,1056]{2,3,0,1:T(8,128)(2,1)S(1)}, bf16[2,2,128,1056]{2,3,0,1:T(8,128)(2,1)S(1)}, u32[]{:S(2)}, u32[]{:S(2)}) collective-permute-start(bf16[2,2,128,1056]{2,3,0,1:T(8,128)(2,1)S(1)} %add_convert_fusion.1), channel_id=1, source_target_pairs={{0,8},{4,12},{8,0},{12,4},{1,9},{5,13},{9,1},{13,5},{2,10},{6,14},... | collective-permute-start | bytes 3244040 | tf_op jit(solution)/shard_map/ppermute | solution.py:38
  67.2 0.1 copy.18
  67.3 0.1 copy.23
  67.5 2.2 %fusion.47 = (f32[128,1056]{0,1:T(8,128)S(1)}, f32[128,1056]{0,1:T(8,128)S(1)}) fusion(s32[128]{0:T(128)S(1)} %add_add_fusion, s32[1056]{0:T(1024)S(1)} %copy-done.28), kind=kLoop, calls=%fused_computation.85 | loop fusion | flops 2027520 | bytes 1086080 | tf_op jit(solution)/shard_map/cos | solution.py:46
  69.7 44.7 %collective-permute-done.3 = bf16[2,2,128,1056]{2,3,0,1:T(8,128)(2,1)S(1)} collective-permute-done((bf16[2,2,128,1056]{2,3,0,1:T(8,128)(2,1)S(1)}, bf16[2,2,128,1056]{2,3,0,1:T(8,128)(2,1)S(1)}, u32[]{:S(2)}, u32[]{:S(2)}) %collective-permute-start.3) | collective-permute-done | bytes 1081376 | tf_op jit(solution)/shard_map/ppermute | solution.py:38
  114.4 0.5 convolution_bitcast_fusion.2
  114.9 0.3 copy-done.5
  115.3 0.5 fusion.4
  115.8 0.3 multiply_subtract_fusion.1
  116.1 0.4 copy-done.31
  116.5 0.3 fusion.7
  116.9 4.6 %add_convert_fusion.2 = bf16[2,2,128,1040]{2,3,0,1:T(8,128)(2,1)S(1)} fusion(bf16[2,2,128,1056]{2,3,0,1:T(8,128)(2,1)S(1)} %fusion.7, f32[128]{0:T(128)S(1)} %get-tuple-element.101, f32[128]{0:T(128)S(1)} %get-tuple-element.102, f32[128]{0:T(128)S(1)} %get-tuple-element.103, f32[128]{0:T(128)S(1)} %get-tuple-element.104, f32[128]{0:T(128)S(1)} %get-tuple-element.105, ...), kind=kLoop, calls=%fused_computation.20 | loop fusion | flops 27156480 | bytes 19177984 | tf_op jit(solution)/shard_map/convert_element_type | solution.py:78
  121.4 0.8 collective-permute-start.4
  122.3 2.2 %fusion.49 = (f32[128,1040]{0,1:T(8,128)S(1)}, f32[128,1040]{0,1:T(8,128)S(1)}) fusion(s32[128]{0:T(128)S(1)} %copy-done.62, s32[1040]{0:T(1024)S(1)} %copy-done.29), kind=kLoop, calls=%fused_computation.87 | loop fusion | flops 1996800 | bytes 1069632 | tf_op jit(solution)/shard_map/cos | solution.py:46
  124.5 22.0 %collective-permute-done.4 = bf16[2,2,128,1040]{2,3,0,1:T(8,128)(2,1)S(1)} collective-permute-done((bf16[2,2,128,1040]{2,3,0,1:T(8,128)(2,1)S(1)}, bf16[2,2,128,1040]{2,3,0,1:T(8,128)(2,1)S(1)}, u32[]{:S(2)}, u32[]{:S(2)}) %collective-permute-start.4) | collective-permute-done | bytes 1064992 | tf_op jit(solution)/shard_map/ppermute | solution.py:38
  146.5 0.5 convolution_bitcast_fusion
  146.9 0.5 fusion.5
  147.5 0.3 multiply_subtract_fusion.2
  147.8 0.4 copy-done.32
  148.2 0.3 fusion.8
  148.5 4.7 %add_convert_fusion.3 = bf16[2,2,128,1024]{2,3,0,1:T(8,128)(2,1)S(1)} fusion(bf16[2,2,128,1040]{2,3,0,1:T(8,128)(2,1)S(1)} %fusion.8, f32[128]{0:T(128)S(1)} %get-tuple-element.84, f32[128]{0:T(128)S(1)} %get-tuple-element.85, f32[128]{0:T(128)S(1)} %get-tuple-element.86, f32[128]{0:T(128)S(1)} %get-tuple-element.87, f32[128]{0:T(128)S(1)} %get-tuple-element.88, ...), kind=kLoop, calls=%fused_computation.25 | loop fusion | flops 26738688 | bytes 18883072 | tf_op jit(solution)/shard_map/convert_element_type | solution.py:78
  153.3 2.9 %collective-permute-start.5 = (bf16[2,2,128,1024]{2,3,0,1:T(8,128)(2,1)S(1)}, bf16[2,2,128,1024]{2,3,0,1:T(8,128)(2,1)S(1)}, u32[]{:S(2)}, u32[]{:S(2)}) collective-permute-start(bf16[2,2,128,1024]{2,3,0,1:T(8,128)(2,1)S(1)} %add_convert_fusion.3), channel_id=1, source_target_pairs={{0,8},{4,12},{8,0},{12,4},{1,9},{5,13},{9,1},{13,5},{2,10},{6,14},... | collective-permute-start | bytes 3145736 | tf_op jit(solution)/shard_map/ppermute | solution.py:38
  156.3 2.1 %fusion.51 = (f32[128,1024]{0,1:T(8,128)S(1)}, f32[128,1024]{0,1:T(8,128)S(1)}) fusion(s32[128]{0:T(128)S(1)} %add_add_fusion, s32[1024]{0:T(1024)S(1)} %iota_add_fusion.11), kind=kLoop, calls=%fused_computation.89 | loop fusion | flops 1966080 | bytes 1053184 | tf_op jit(solution)/shard_map/cos | solution.py:46
  158.4 43.0 %collective-permute-done.5 = bf16[2,2,128,1024]{2,3,0,1:T(8,128)(2,1)S(1)} collective-permute-done((bf16[2,2,128,1024]{2,3,0,1:T(8,128)(2,1)S(1)}, bf16[2,2,128,1024]{2,3,0,1:T(8,128)(2,1)S(1)}, u32[]{:S(2)}, u32[]{:S(2)}) %collective-permute-start.5) | collective-permute-done | bytes 1048608 | tf_op jit(solution)/shard_map/ppermute | solution.py:38
  201.5 0.5 fusion.26
  201.9 0.5 fusion.10
  202.5 0.3 multiply_subtract_fusion.3
  202.8 0.3 fusion.9
  203.1 1.3 copy.13
  (152 shorter events, 1.1 us)
Async XLA Ops:
  0.0 6.1 %copy-start = (bf16[4,2,2,2,128,128]{5,4,3,2,1,0:T(8,128)(2,1)S(1)}, bf16[4,2,2,2,128,128]{5,4,3,2,1,0:T(8,128)(2,1)}, u32[]{:S(2)}) copy-start(bf16[4,2,2,2,128,128]{5,4,3,2,1,0:T(8,128)(2,1)} %param.5) | copy-start | bytes 3145732
  0.0 8.8 %copy-start.63 = (f32[4,4]{1,0:T(4,128)S(1)}, f32[4,4]{1,0:T(4,128)}, u32[]{:S(2)}) copy-start(f32[4,4]{1,0:T(4,128)} %param.6) | copy-start | bytes 196
  0.0 8.8 %copy-start.60 = (s32[4,2,128]{2,1,0:T(2,128)S(1)}, s32[4,2,128]{2,1,0:T(2,128)}, u32[]{:S(2)}) copy-start(s32[4,2,128]{2,1,0:T(2,128)} %param.7) | copy-start | bytes 12292
  1.7 15.4 %collective-permute-start.1 = (bf16[2,2,128,32]{2,3,1,0:T(8,128)(2,1)S(1)}, bf16[2,2,128,32]{2,3,1,0:T(8,128)(2,1)S(1)}, u32[]{:S(2)}, u32[]{:S(2)}) collective-permute-start(bf16[2,2,128,32]{2,3,1,0:T(8,128)(2,1)S(1)} %get-tuple-element.50), channel_id=1, source_target_pairs={{1,0},{2,1},{3,2},{5,4},{6,5},{7,6},{9,8},{10,9},{11,10},{13,12},{... | collective-permute-start | bytes 98312 | tf_op jit(solution)/shard_map/ppermute | solution.py:28
  3.0 14.2 %collective-permute-start = (bf16[2,2,128,32]{2,3,1,0:T(8,128)(2,1)S(1)}, bf16[2,2,128,32]{2,3,1,0:T(8,128)(2,1)S(1)}, u32[]{:S(2)}, u32[]{:S(2)}) collective-permute-start(bf16[2,2,128,32]{2,3,1,0:T(8,128)(2,1)S(1)} %get-tuple-element.49), channel_id=1, source_target_pairs={{0,1},{1,2},{2,3},{4,5},{5,6},{6,7},{8,9},{9,10},{10,11},{12,13},{... | collective-permute-start | bytes 98312 | tf_op jit(solution)/shard_map/ppermute | solution.py:26
  6.2 10.9 %copy-start.2 = (bf16[1,2,2,2,128,128]{5,4,3,2,1,0:T(8,128)(2,1)}, bf16[1,2,2,2,128,128]{5,4,3,2,1,0:T(8,128)(2,1)S(1)}, u32[]{:S(2)}) copy-start(bf16[1,2,2,2,128,128]{5,4,3,2,1,0:T(8,128)(2,1)S(1)} %get-tuple-element.48) | copy-start | bytes 786436
  6.3 11.0 %copy-start.1 = (bf16[1,2,2,2,128,128]{5,4,3,2,1,0:T(8,128)(2,1)}, bf16[1,2,2,2,128,128]{5,4,3,2,1,0:T(8,128)(2,1)S(1)}, u32[]{:S(2)}) copy-start(bf16[1,2,2,2,128,128]{5,4,3,2,1,0:T(8,128)(2,1)S(1)} %get-tuple-element.45) | copy-start | bytes 786436
  12.5 10.1 %copy-start.34 = (f32[128]{0:T(128)}, f32[128]{0:T(128)S(1)}, u32[]{:S(2)}) copy-start(f32[128]{0:T(128)S(1)} %get-tuple-element.134) | copy-start | bytes 1540
  12.5 10.1 %copy-start.35 = (f32[128]{0:T(128)}, f32[128]{0:T(128)S(1)}, u32[]{:S(2)}) copy-start(f32[128]{0:T(128)S(1)} %get-tuple-element.135) | copy-start | bytes 1540
  12.5 10.1 %copy-start.36 = (f32[128]{0:T(128)}, f32[128]{0:T(128)S(1)}, u32[]{:S(2)}) copy-start(f32[128]{0:T(128)S(1)} %get-tuple-element.136) | copy-start | bytes 1540
  12.5 10.1 %copy-start.37 = (f32[128]{0:T(128)}, f32[128]{0:T(128)S(1)}, u32[]{:S(2)}) copy-start(f32[128]{0:T(128)S(1)} %get-tuple-element.137) | copy-start | bytes 1540
  12.5 10.1 %copy-start.38 = (f32[128]{0:T(128)}, f32[128]{0:T(128)S(1)}, u32[]{:S(2)}) copy-start(f32[128]{0:T(128)S(1)} %get-tuple-element.138) | copy-start | bytes 1540
  12.6 10.1 %copy-start.39 = (f32[128]{0:T(128)}, f32[128]{0:T(128)S(1)}, u32[]{:S(2)}) copy-start(f32[128]{0:T(128)S(1)} %get-tuple-element.139) | copy-start | bytes 1540
  12.6 10.1 %copy-start.40 = (f32[128]{0:T(128)}, f32[128]{0:T(128)S(1)}, u32[]{:S(2)}) copy-start(f32[128]{0:T(128)S(1)} %get-tuple-element.140) | copy-start | bytes 1540
  12.6 10.1 %copy-start.41 = (f32[128]{0:T(128)}, f32[128]{0:T(128)S(1)}, u32[]{:S(2)}) copy-start(f32[128]{0:T(128)S(1)} %get-tuple-element.141) | copy-start | bytes 1540
  17.1 0.7 copy-start.46
  17.1 0.7 copy-start.48
  17.1 0.7 copy-start.50
  17.8 8.0 %copy-start.14 = (f32[128,17]{1,0:T(8,128)S(1)}, f32[128,17]{1,0:T(8,128)}, u32[]{:S(2)}) copy-start(f32[128,17]{1,0:T(8,128)} %get-tuple-element.15) | copy-start | bytes 26116
  17.8 8.1 %copy-start.13 = (f32[128,17]{1,0:T(8,128)S(1)}, f32[128,17]{1,0:T(8,128)}, u32[]{:S(2)}) copy-start(f32[128,17]{1,0:T(8,128)} %get-tuple-element.16) | copy-start | bytes 26116
  17.8 9.7 %copy-start.30 = (s32[1072]{0:T(1024)S(1)}, s32[1072]{0:T(1024)}, u32[]{:S(2)}) copy-start(s32[1072]{0:T(1024)} %iota_add_fusion.8) | copy-start | bytes 12868
  17.8 32.5 %copy-start.43 = (f32[128]{0:T(128)S(1)}, f32[128]{0:T(128)}, u32[]{:S(2)}) copy-start(f32[128]{0:T(128)} %get-tuple-element.142) | copy-start | bytes 1540
  17.9 32.5 %copy-start.45 = (f32[128]{0:T(128)S(1)}, f32[128]{0:T(128)}, u32[]{:S(2)}) copy-start(f32[128]{0:T(128)} %get-tuple-element.143) | copy-start | bytes 1540
  17.9 32.5 %copy-start.47 = (f32[128]{0:T(128)S(1)}, f32[128]{0:T(128)}, u32[]{:S(2)}) copy-start(f32[128]{0:T(128)} %get-tuple-element.144) | copy-start | bytes 1540
  17.9 32.5 %copy-start.49 = (f32[128]{0:T(128)S(1)}, f32[128]{0:T(128)}, u32[]{:S(2)}) copy-start(f32[128]{0:T(128)} %get-tuple-element.145) | copy-start | bytes 1540
  17.9 32.5 %copy-start.51 = (f32[128]{0:T(128)S(1)}, f32[128]{0:T(128)}, u32[]{:S(2)}) copy-start(f32[128]{0:T(128)} %get-tuple-element.146) | copy-start | bytes 1540
  17.9 32.5 %copy-start.53 = (f32[128]{0:T(128)S(1)}, f32[128]{0:T(128)}, u32[]{:S(2)}) copy-start(f32[128]{0:T(128)} %get-tuple-element.147) | copy-start | bytes 1540
  17.9 32.5 %copy-start.55 = (f32[128]{0:T(128)S(1)}, f32[128]{0:T(128)}, u32[]{:S(2)}) copy-start(f32[128]{0:T(128)} %get-tuple-element.148) | copy-start | bytes 1540
  17.9 32.5 %copy-start.57 = (f32[128]{0:T(128)S(1)}, f32[128]{0:T(128)}, u32[]{:S(2)}) copy-start(f32[128]{0:T(128)} %get-tuple-element.149) | copy-start | bytes 1540
  17.9 32.5 %copy-start.59 = (f32[128]{0:T(128)S(1)}, f32[128]{0:T(128)}, u32[]{:S(2)}) copy-start(f32[128]{0:T(128)} %get-tuple-element.150) | copy-start | bytes 1540
  22.7 27.6 %collective-permute-start.2 = (bf16[2,2,128,1072]{2,3,1,0:T(8,128)(2,1)S(1)}, bf16[2,2,128,1072]{2,3,1,0:T(8,128)(2,1)S(1)}, u32[]{:S(2)}, u32[]{:S(2)}) collective-permute-start(bf16[2,2,128,1072]{2,3,1,0:T(8,128)(2,1)S(1)} %add_convert_fusion), channel_id=1, source_target_pairs={{0,4},{4,0},{8,12},{12,8},{1,5},{5,1},{9,13},{13,9},{2,6},{6,2},{1... | collective-permute-start | bytes 3293192 | tf_op jit(solution)/shard_map/ppermute | solution.py:38
  25.9 30.4 %copy-start.61 = (s32[128]{0:T(128)}, s32[128]{0:T(128)S(1)}, u32[]{:S(2)}) copy-start(s32[128]{0:T(128)S(1)} %add_add_fusion.1) | copy-start | bytes 1540
  29.8 26.5 %copy-start.15 = (bf16[1,2,128,128]{3,2,1,0:T(8,128)(2,1)S(1)}, bf16[1,2,128,128]{3,2,1,0:T(8,128)(2,1)}, u32[]{:S(2)}) copy-start(bf16[1,2,128,128]{3,2,1,0:T(8,128)(2,1)} %get-tuple-element.81) | copy-start | bytes 196612
  29.8 26.5 %copy-start.16 = (bf16[1,2,128,128]{3,2,1,0:T(8,128)(2,1)S(1)}, bf16[1,2,128,128]{3,2,1,0:T(8,128)(2,1)}, u32[]{:S(2)}) copy-start(bf16[1,2,128,128]{3,2,1,0:T(8,128)(2,1)} %get-tuple-element.82) | copy-start | bytes 196612
  56.2 0.8 copy-start.7
  56.2 0.9 copy-start.8
  57.6 0.7 copy-start.33
  58.6 8.5 %copy-start.12 = (f32[128,17]{1,0:T(8,128)S(1)}, f32[128,17]{1,0:T(8,128)}, u32[]{:S(2)}) copy-start(f32[128,17]{1,0:T(8,128)} %get-tuple-element.13) | copy-start | bytes 26116
  58.6 8.5 %copy-start.11 = (f32[128,17]{1,0:T(8,128)S(1)}, f32[128,17]{1,0:T(8,128)}, u32[]{:S(2)}) copy-start(f32[128,17]{1,0:T(8,128)} %get-tuple-element.14) | copy-start | bytes 26116
  58.6 8.6 %copy-start.10 = (f32[128,17]{1,0:T(8,128)S(1)}, f32[128,17]{1,0:T(8,128)}, u32[]{:S(2)}) copy-start(f32[128,17]{1,0:T(8,128)} %get-tuple-element.6) | copy-start | bytes 26116
  58.6 8.7 %copy-start.9 = (f32[128,17]{1,0:T(8,128)S(1)}, f32[128,17]{1,0:T(8,128)}, u32[]{:S(2)}) copy-start(f32[128,17]{1,0:T(8,128)} %get-tuple-element.5) | copy-start | bytes 26116
  58.6 8.8 %copy-start.22 = (bf16[1,128,128]{2,1,0:T(8,128)(2,1)S(1)}, bf16[1,128,128]{2,1,0:T(8,128)(2,1)}, u32[]{:S(2)}) copy-start(bf16[1,128,128]{2,1,0:T(8,128)(2,1)} %get-tuple-element.183) | copy-start | bytes 98308
  58.6 8.8 %copy-start.23 = (bf16[1,128,128]{2,1,0:T(8,128)(2,1)S(1)}, bf16[1,128,128]{2,1,0:T(8,128)(2,1)}, u32[]{:S(2)}) copy-start(bf16[1,128,128]{2,1,0:T(8,128)(2,1)} %get-tuple-element.184) | copy-start | bytes 98308
  58.6 8.8 %copy-start.27 = (bf16[1,128,128]{2,1,0:T(8,128)(2,1)S(1)}, bf16[1,128,128]{2,1,0:T(8,128)(2,1)}, u32[]{:S(2)}) copy-start(bf16[1,128,128]{2,1,0:T(8,128)(2,1)} %get-tuple-element.179) | copy-start | bytes 98308
  58.7 8.8 %copy-start.28 = (s32[1056]{0:T(1024)S(1)}, s32[1056]{0:T(1024)}, u32[]{:S(2)}) copy-start(s32[1056]{0:T(1024)} %iota_add_fusion.9) | copy-start | bytes 12676
  58.7 55.7 %copy-start.3 = (bf16[1,2,128,128]{3,2,1,0:T(8,128)(2,1)S(1)}, bf16[1,2,128,128]{3,2,1,0:T(8,128)(2,1)}, u32[]{:S(2)}) copy-start(bf16[1,2,128,128]{3,2,1,0:T(8,128)(2,1)} %get-tuple-element.77) | copy-start | bytes 196612
  58.7 55.7 %copy-start.4 = (bf16[1,2,128,128]{3,2,1,0:T(8,128)(2,1)S(1)}, bf16[1,2,128,128]{3,2,1,0:T(8,128)(2,1)}, u32[]{:S(2)}) copy-start(bf16[1,2,128,128]{3,2,1,0:T(8,128)(2,1)} %get-tuple-element.78) | copy-start | bytes 196612
  63.5 50.9 %collective-permute-start.3 = (bf16[2,2,128,1056]{2,3,0,1:T(8,128)(2,1)S(1)}, bf16[2,2,128,1056]{2,3,0,1:T(8,128)(2,1)S(1)}, u32[]{:S(2)}, u32[]{:S(2)}) collective-permute-start(bf16[2,2,128,1056]{2,3,0,1:T(8,128)(2,1)S(1)} %add_convert_fusion.1), channel_id=1, source_target_pairs={{0,8},{4,12},{8,0},{12,4},{1,9},{5,13},{9,1},{13,5},{2,10},{6,14},... | collective-permute-start | bytes 3244040 | tf_op jit(solution)/shard_map/ppermute | solution.py:38
  114.4 0.8 copy-start.5
  114.4 0.9 copy-start.6
  115.8 0.7 copy-start.31
  116.8 5.4 %copy-start.20 = (bf16[1,128,128]{2,1,0:T(8,128)(2,1)S(1)}, bf16[1,128,128]{2,1,0:T(8,128)(2,1)}, u32[]{:S(2)}) copy-start(bf16[1,128,128]{2,1,0:T(8,128)(2,1)} %get-tuple-element.185) | copy-start | bytes 98308
  116.8 5.4 %copy-start.21 = (bf16[1,128,128]{2,1,0:T(8,128)(2,1)S(1)}, bf16[1,128,128]{2,1,0:T(8,128)(2,1)}, u32[]{:S(2)}) copy-start(bf16[1,128,128]{2,1,0:T(8,128)(2,1)} %get-tuple-element.186) | copy-start | bytes 98308
  116.8 5.4 %copy-start.26 = (bf16[1,128,128]{2,1,0:T(8,128)(2,1)S(1)}, bf16[1,128,128]{2,1,0:T(8,128)(2,1)}, u32[]{:S(2)}) copy-start(bf16[1,128,128]{2,1,0:T(8,128)(2,1)} %get-tuple-element.180) | copy-start | bytes 98308
  116.8 5.5 %copy-start.29 = (s32[1040]{0:T(1024)S(1)}, s32[1040]{0:T(1024)}, u32[]{:S(2)}) copy-start(s32[1040]{0:T(1024)} %iota_add_fusion.10) | copy-start | bytes 12484
  116.8 5.5 %copy-start.62 = (s32[128]{0:T(128)S(1)}, s32[128]{0:T(128)}, u32[]{:S(2)}) copy-start(s32[128]{0:T(128)} %copy-done.61) | copy-start | bytes 1540
  121.4 25.0 %collective-permute-start.4 = (bf16[2,2,128,1040]{2,3,0,1:T(8,128)(2,1)S(1)}, bf16[2,2,128,1040]{2,3,0,1:T(8,128)(2,1)S(1)}, u32[]{:S(2)}, u32[]{:S(2)}) collective-permute-start(bf16[2,2,128,1040]{2,3,0,1:T(8,128)(2,1)S(1)} %add_convert_fusion.2), channel_id=1, source_target_pairs={{0,4},{4,0},{8,12},{12,8},{1,5},{5,1},{9,13},{13,9},{2,6},{6,2},{1... | collective-permute-start | bytes 3194888 | tf_op jit(solution)/shard_map/ppermute | solution.py:38
  147.5 0.7 copy-start.32
  148.5 7.7 %copy-start.18 = (bf16[1,128,128]{2,1,0:T(8,128)(2,1)S(1)}, bf16[1,128,128]{2,1,0:T(8,128)(2,1)}, u32[]{:S(2)}) copy-start(bf16[1,128,128]{2,1,0:T(8,128)(2,1)} %get-tuple-element.51) | copy-start | bytes 98308
  148.5 7.7 %copy-start.19 = (bf16[1,128,128]{2,1,0:T(8,128)(2,1)S(1)}, bf16[1,128,128]{2,1,0:T(8,128)(2,1)}, u32[]{:S(2)}) copy-start(bf16[1,128,128]{2,1,0:T(8,128)(2,1)} %get-tuple-element.52) | copy-start | bytes 98308
  148.5 7.7 %copy-start.25 = (bf16[1,128,128]{2,1,0:T(8,128)(2,1)S(1)}, bf16[1,128,128]{2,1,0:T(8,128)(2,1)}, u32[]{:S(2)}) copy-start(bf16[1,128,128]{2,1,0:T(8,128)(2,1)} %get-tuple-element.54) | copy-start | bytes 98308
  148.5 7.8 %copy-start.17 = (bf16[1,128,128]{2,1,0:T(8,128)(2,1)S(1)}, bf16[1,128,128]{2,1,0:T(8,128)(2,1)}, u32[]{:S(2)}) copy-start(bf16[1,128,128]{2,1,0:T(8,128)(2,1)} %get-tuple-element.20) | copy-start | bytes 98308
  148.5 7.8 %copy-start.24 = (bf16[1,128,128]{2,1,0:T(8,128)(2,1)S(1)}, bf16[1,128,128]{2,1,0:T(8,128)(2,1)}, u32[]{:S(2)}) copy-start(bf16[1,128,128]{2,1,0:T(8,128)(2,1)} %get-tuple-element.53) | copy-start | bytes 98308
  153.3 48.2 %collective-permute-start.5 = (bf16[2,2,128,1024]{2,3,0,1:T(8,128)(2,1)S(1)}, bf16[2,2,128,1024]{2,3,0,1:T(8,128)(2,1)S(1)}, u32[]{:S(2)}, u32[]{:S(2)}) collective-permute-start(bf16[2,2,128,1024]{2,3,0,1:T(8,128)(2,1)S(1)} %add_convert_fusion.3), channel_id=1, source_target_pairs={{0,8},{4,12},{8,0},{12,4},{1,9},{5,13},{9,1},{13,5},{2,10},{6,14},... | collective-permute-start | bytes 3145736 | tf_op jit(solution)/shard_map/ppermute | solution.py:38
  (6 other events, 3.8 us)
where the time goes:
time: 205 us; the launch traced here: 204 us
  waiting for transfers between devices  130 us (63%)
  other arithmetic  46.6 us (23%)
  starting transfers between devices  14.7 us (7%)
  local copies, waits for them, and re-layouts  7.68 us (4%)
  matrix products  4.05 us (2%)
    ppermute x4, waiting for transfers between devices, from_partner(): return lax.ppermute(value, axis, pairs)  130 us
    convert_element_type x4, other arithmetic, interpolate(): return total.astype(jnp.bfloat16)  18.8 us
    ppermute x4, starting transfers between devices, from_partner(): return lax.ppermute(value, axis, pairs)  10.4 us
    cos x4, other arithmetic, rotate(): cosine = jnp.cos(phase)  8.68 us
    select_n x1, other arithmetic, on_device(): lower_rows = jnp.where(own_half == 0, own_rows, partner)  5.82 us
    unnamed x129, local copies, waits for them, and re-layouts  4.3 us
  transfers between devices with their start and end apart: 6, of which 4 were waited for; matrix products, arithmetic and copies ran while one was open for 11% of the time, Pallas kernels for 0%

commit v1 on v0

v1 whole, which is shorter than its diff:
```python
import functools
import math

import jax
import jax.numpy as jnp
import numpy as np
from jax import lax
from jax.experimental import pallas as pl
from jax.experimental.pallas import tpu as pltpu
from jax.sharding import PartitionSpec as P

ANGLES = 128
RIM = 8
TAPS = 4
LEVELS = 4
LANES = 128
PERIOD = 64
ROWS = 32


def phases_of(bit_count):
    runs = []
    for level in range(LEVELS):
        bit = level % bit_count
        if runs and len(set(runs[-1][1] + [bit])) <= 2:
            runs[-1][0].append(level)
            runs[-1][1].append(bit)
        else:
            runs.append(([level], [bit]))
    return [(levels, bits, sorted(set(bits))) for levels, bits in runs]


def phase_table(levels, margin):
    cols = np.arange(LANES, dtype=np.int64) - margin
    rows = np.arange(2 * ANGLES, dtype=np.int64) + 1
    out = []
    for level in levels:
        wrapped = (cols[None, :] * rows[:, None] * (7 + level)) % PERIOD
        phase = wrapped.astype(np.float64) * (2.0 * math.pi / PERIOD)
        out.append(np.stack([np.cos(phase), np.sin(phase)]).reshape(2, 2, ANGLES, LANES))
    return np.stack(out).astype(np.float32)


def shift_masks(range_shifts):
    steps = range_shifts + RIM
    bits = [(steps >> k) & 1 for k in range(3)] + [1 - ((steps >> 3) & 1)]
    return jnp.stack(bits, axis=-1)


def merge_kernel(start_ref, taps_ref, masks_ref, weights_ref, table_ref, in_ref, out_ref,
                 x_ref, y_ref, w_ref, *, places, margin, total):
    members, _, wide = x_ref.shape
    given = in_ref.shape[-1]
    width = out_ref.shape[-1]
    start = start_ref[0]
    n_levels = len(places)
    x_ref[:, :, wide - LANES:] = jnp.zeros((members, 2 * ANGLES, LANES), jnp.bfloat16)
    x_ref[:, :, 0:given] = in_ref[...]
    for level in range(n_levels):
        place = places[level]
        for h in range(2):
            for e in range(2):
                real = weights_ref[level, e, h, 0]
                imag = weights_ref[level, e, h, 1]
                r0, c0 = h * 2 * ANGLES, e * 2 * ANGLES
                w_ref[r0:r0 + ANGLES, c0:c0 + ANGLES] = real
                w_ref[r0:r0 + ANGLES, c0 + ANGLES:c0 + 2 * ANGLES] = -imag
                w_ref[r0 + ANGLES:r0 + 2 * ANGLES, c0:c0 + ANGLES] = imag
                w_ref[r0 + ANGLES:r0 + 2 * ANGLES, c0 + ANGLES:c0 + 2 * ANGLES] = real
        taps = [taps_ref[level, t] for t in range(TAPS)]

        for side in range(2):
            own = [p for p in range(members) if (p >> place) % 2 == side]

            def rows_step(block, carry, side=side, own=own, level=level, taps=taps):
                flags = masks_ref[level, side, pl.ds(pl.multiple_of(block * ROWS, ROWS), ROWS), :]
                masks = [jnp.broadcast_to(flags[:, k:k + 1], (ROWS, wide)) != 0 for k in range(4)]
                for p in own:
                    for c in range(2):
                        rows = pl.ds(pl.multiple_of(c * ANGLES + block * ROWS, ROWS), ROWS)
                        cells = x_ref[p, rows, :].astype(jnp.float32)
                        after = pltpu.roll(cells, wide - 1, 1)
                        first = taps[0] * cells + taps[1] * after
                        second = taps[2] * cells + taps[3] * after
                        v = first + pltpu.roll(second, wide - 2, 1)
                        for k, by in ((0, wide - 1), (1, wide - 2), (2, wide - 4), (3, RIM)):
                            v = jnp.where(masks[k], pltpu.roll(v, by, 1), v)
                        y_ref[p, rows, :] = v.astype(jnp.bfloat16)
                return carry

            lax.fori_loop(0, ANGLES // ROWS, rows_step, 0)

        last = level == n_levels - 1
        cols = start + lax.broadcasted_iota(jnp.int32, (ANGLES, LANES), 1)
        for low in [p for p in range(members) if (p >> place) % 2 == 0]:
            high = low + 2 ** place
            for h in range(2):
                r0 = h * 2 * ANGLES
                z = jnp.dot(w_ref[r0:r0 + 2 * ANGLES, 0:2 * ANGLES], y_ref[low], preferred_element_type=jnp.float32)
                z = z + jnp.dot(w_ref[r0:r0 + 2 * ANGLES, 2 * ANGLES:], y_ref[high], preferred_element_type=jnp.float32)
                dest = high if h else low
                cosine = table_ref[level, 0, h]
                sinus = table_ref[level, 1, h]
                for tile in range(wide // LANES):
                    at = tile * LANES
                    zr = z[:ANGLES, at:at + LANES]
                    zi = z[ANGLES:, at:at + LANES]
                    re = zr * cosine - zi * sinus
                    im = zr * sinus + zi * cosine
                    if not last and (at < margin or at + LANES > given - margin):
                        inside = jnp.logical_and(cols + at >= 0, cols + at < total)
                        re = jnp.where(inside, re, 0.0)
                        im = jnp.where(inside, im, 0.0)
                    x_ref[dest, 0:ANGLES, at:at + LANES] = re.astype(jnp.bfloat16)
                    x_ref[dest, ANGLES:, at:at + LANES] = im.astype(jnp.bfloat16)
    for p in range(members):
        v = x_ref[p].astype(jnp.float32)
        out_ref[p] = pltpu.roll(v, wide - margin, 1)[:, :width].astype(jnp.bfloat16)


def merge_levels(start, taps, masks, weights, table, pieces, places, margin, total):
    members, rows, given = pieces.shape
    width = given - 2 * margin
    wide = -(-given // LANES) * LANES
    smem = pl.BlockSpec(memory_space=pltpu.SMEM)
    vmem = pl.BlockSpec(memory_space=pltpu.VMEM)
    return pl.pallas_call(
        functools.partial(merge_kernel, places=places, margin=margin, total=total),
        out_shape=jax.ShapeDtypeStruct((members, rows, width), jnp.bfloat16),
        in_specs=[smem, smem, vmem, vmem, vmem, vmem],
        out_specs=vmem,
        scratch_shapes=[
            pltpu.VMEM((members, rows, wide), jnp.bfloat16),
            pltpu.VMEM((members, rows, wide), jnp.bfloat16),
            pltpu.VMEM((4 * ANGLES, 4 * ANGLES), jnp.bfloat16),
        ],
        compiler_params=pltpu.CompilerParams(vmem_limit_bytes=48 * 2**20),
        name="merge_levels",
    )(start, taps, masks, weights, table, pieces)


def with_halo(cells, axis, margin):
    count = lax.axis_size(axis)
    head = cells[..., :margin]
    tail = cells[..., cells.shape[-1] - margin:]
    left = lax.ppermute(tail, axis, [(i, i + 1) for i in range(count - 1)])
    right = lax.ppermute(head, axis, [(i + 1, i) for i in range(count - 1)])
    return jnp.concatenate([left, cells, right], axis=-1)


def on_device(image, interp_weights, range_taps, range_shifts):
    _, groups, _, range_width = image.shape
    sub_count = lax.axis_size("sub")
    total = range_width * lax.axis_size("rng")
    sub_index = lax.axis_index("sub")
    masks = shift_masks(range_shifts)
    current = image
    for levels, bits, distinct in phases_of(sub_count.bit_length() - 1):
        members = 2 ** len(distinct)
        parts = members // groups
        width = range_width // parts
        margin = len(levels) * RIM
        first, end = levels[0], levels[-1] + 1
        spread = [sum(((p >> j) & 1) << bit for j, bit in enumerate(distinct)) for p in range(members)]
        bases = [i for i in range(sub_count) if all(not (i >> bit) & 1 for bit in distinct)]
        index_groups = None if len(bases) == 1 else [[base + s for s in spread] for base in bases]
        member = sum(((sub_index >> bit) & 1) << j for j, bit in enumerate(distinct))
        start = lax.axis_index("rng") * range_width + member // groups * width - margin
        padded = with_halo(current, "rng", margin)
        pieces = jnp.stack([
            padded[:, p % groups, :, p // groups * width:p // groups * width + width + 2 * margin]
            for p in range(members)
        ]).reshape(members, 2 * ANGLES, width + 2 * margin)
        pieces = lax.all_to_all(pieces, "sub", 0, 0, axis_index_groups=index_groups, tiled=True)
        merged = merge_levels(
            start.reshape(1).astype(jnp.int32), range_taps[first:end], masks[first:end],
            interp_weights[first:end], jnp.asarray(phase_table(levels, margin)), pieces,
            [distinct.index(bit) for bit in bits], margin, total)
        back = lax.all_to_all(merged, "sub", 0, 0, axis_index_groups=index_groups, tiled=True)
        back = back.reshape(parts, groups, 2, ANGLES, width)
        current = jnp.transpose(back, (2, 1, 3, 0, 4)).reshape(image.shape)
    return current


def solution(mesh):
    return jax.shard_map(
        on_device,
        mesh=mesh,
        in_specs=(P(None, ("img", "sub"), None, "rng"), P(), P(), P()),
        out_specs=P(None, ("img", "sub"), None, "rng"),
        check_vma=False,
    )
```

time: 205 us -> 108 us (0.53)
  waiting for transfers between devices: 130 us -> 28.5 us
  other arithmetic: 46.6 us -> 1.99 us
  blocking collectives: 0 us -> 28.6 us
  Pallas kernels: 0 us -> 27.4 us
  matrix products: 4.05 us -> 0 us
  starting transfers between devices: 14.7 us -> 10.8 us
  local copies, waits for them, and re-layouts: 7.68 us -> 10.4 us
    ppermute x6 -> x2, waiting for transfers between devices: 130 us -> 0.01 us  [the longest x1 0.01 us: with_halo(): right = lax.ppermute(head, axis, [(i + 1, i) for i in range(count - 1)])]
    all_to_all x0 -> x1, blocking collectives: none -> 28.6 us  [on_device(): lax.all_to_all(merged, 'sub', 0, 0, axis_index_groups=index_groups, tiled...]
    all_to_all x0 -> x1, waiting for transfers between devices: none -> 28.4 us  [on_device(): lax.all_to_all(pieces, 'sub', 0, 0, axis_index_groups=index_groups, tiled...]
    pallas_call x0 -> x1, Pallas kernels: none -> 27.4 us  [merge_levels(): pl.pallas_call(functools.partial(merge_kernel, places=places, margin=marg...]
    convert_element_type x8 -> x0, other arithmetic: 20 us -> none  [the longest x4 18.8 us: interpolate(): return total.astype(jnp.bfloat16)]
    ppermute x6 -> x2, starting transfers between devices: 14.7 us -> 4.33 us  [the longest x1 3.04 us: with_halo(): left = lax.ppermute(tail, axis, [(i, i + 1) for i in range(count - 1)])]
    cos x4 -> x0, other arithmetic: 8.68 us -> none  [rotate(): cosine = jnp.cos(phase)]
    all_to_all x0 -> x1, starting transfers between devices: none -> 6.48 us  [on_device(): lax.all_to_all(pieces, 'sub', 0, 0, axis_index_groups=index_groups, tiled...]
  transfers between devices with their start and end apart: 6 -> 3, of which waited for: 4 -> 1; matrix products, arithmetic and copies ran while one was open for 11% -> 3% of each run, Pallas kernels for 0% -> 0%
where the time goes in v1:
time: 108 us
  blocking collectives  28.6 us (26%)
  waiting for transfers between devices  28.5 us (26%)
  Pallas kernels  27.4 us (25%)
  starting transfers between devices  10.8 us (10%)
  local copies, waits for them, and re-layouts  10.4 us (10%)
  other arithmetic  1.99 us (2%)
    all_to_all x1, blocking collectives, on_device(): lax.all_to_all(merged, 'sub', 0, 0, axis_index_groups=index_groups, tiled...  28.6 us
    all_to_all x1, waiting for transfers between devices, on_device(): lax.all_to_all(pieces, 'sub', 0, 0, axis_index_groups=index_groups, tiled...  28.4 us
    pallas_call x1, Pallas kernels, merge_levels(): pl.pallas_call(functools.partial(merge_kernel, places=places, margin=marg...  27.4 us
    all_to_all x1, starting transfers between devices, on_device(): lax.all_to_all(pieces, 'sub', 0, 0, axis_index_groups=index_groups, tiled...  6.48 us
    unnamed x11, local copies, waits for them, and re-layouts  3.05 us
    ppermute x1, starting transfers between devices, with_halo(): left = lax.ppermute(tail, axis, [(i, i + 1) for i in range(count - 1)])  3.04 us
  transfers between devices with their start and end apart: 3, of which 1 were waited for; matrix products, arithmetic and copies ran while one was open for 3% of the time, Pallas kernels for 0%

profile of v1, /device:TPU:0, one launch (start us, length us, event | category | flops | bytes accessed | tf_op | source)
XLA Modules:
  0.0 107.8 jit_solution(15562768828166903200)
XLA Ops:
  0.0 1.1 fusion.1
  1.1 1.3 %collective-permute-start.1 = (bf16[2,2,128,32]{3,2,1,0:T(8,128)(2,1)S(1)}, bf16[2,2,128,32]{3,2,1,0:T(8,128)(2,1)S(1)}, u32[]{:S(2)}, u32[]{:S(2)}) collective-permute-start(bf16[2,2,128,32]{3,2,1,0:T(8,128)(2,1)S(1)} %get-tuple-element.10), channel_id=1, source_target_pairs={{1,0},{2,1},{3,2},{5,4},{6,5},{7,6},{9,8},{10,9},{11,10},{13,12},{... | collective-permute-start | bytes 98312 | tf_op jit(solution)/shard_map/ppermute | solution.py:147
  2.4 3.0 %collective-permute-start = (bf16[2,2,128,32]{3,2,1,0:T(8,128)(2,1)S(1)}, bf16[2,2,128,32]{3,2,1,0:T(8,128)(2,1)S(1)}, u32[]{:S(2)}, u32[]{:S(2)}) collective-permute-start(bf16[2,2,128,32]{3,2,1,0:T(8,128)(2,1)S(1)} %get-tuple-element.9), channel_id=1, source_target_pairs={{0,1},{1,2},{2,3},{4,5},{5,6},{6,7},{8,9},{9,10},{10,11},{12,13},{... | collective-permute-start | bytes 98312 | tf_op jit(solution)/shard_map/ppermute | solution.py:146
  5.4 1.3 %constant_dynamic-update-slice_fusion.1 = bf16[2,2,128,1056]{3,2,1,0:T(8,128)(2,1)S(1)} fusion(bf16[2,2,128,1024]{3,2,1,0:T(8,128)(2,1)} %param.5), kind=kLoop, calls=%fused_computation.5 | loop fusion | bytes 2097152
  6.7 0.0 collective-permute-done.1
  6.8 0.0 copy-start.3
  6.8 0.4 fusion
  7.2 0.2 copy.50
  7.3 0.2 copy.51
  7.5 0.0 collective-permute-done
  7.5 0.5 copy-done.3
  8.0 0.3 pad_maximum_fusion.2
  8.4 0.2 copy.48
  8.5 0.2 copy.49
  8.7 1.2 %pad_maximum_fusion = bf16[4,256,576]{1,2,0:T(8,128)(2,1)} fusion(bf16[1,256,576]{1,2,0:T(8,128)(2,1)S(1)} %copy.51, bf16[1,256,576]{1,2,0:T(8,128)(2,1)S(1)} %copy.50, bf16[1,256,576]{1,2,0:T(8,128)(2,1)S(1)} %copy.49, bf16[1,256,576]{1,2,0:T(8,128)(2,1)S(1)} %copy.48), kind=kLoop, calls=%fused_computation | loop fusion | flops 1769472 | bytes 2359296 | tf_op jit(solution)/shard_map/stack | solution.py:170
  9.9 0.0 copy-start.4
  9.9 6.5 %all-to-all-start = ((bf16[4,256,576]{1,2,0:T(8,128)(2,1)}), bf16[4,256,576]{1,2,0:T(8,128)(2,1)}, u32[]{:S(2)}, u32[]{:S(2)}) async-start(bf16[4,256,576]{1,2,0:T(8,128)(2,1)} %pad_maximum_fusion), calls=%async_computation | async-start | bytes 2359296 | tf_op jit(solution)/shard_map/all_to_all | solution.py:174
  16.3 0.0 copy-done.4
  16.4 0.2 copy.38
  16.6 0.2 copy.39
  16.8 0.2 copy.40
  17.1 0.2 copy.41
  17.3 0.5 pad_add_fusion.masks_ref
  17.8 0.0 copy-start
  17.8 0.0 copy-start.2
  17.8 28.4 %all-to-all-done = bf16[4,256,576]{1,2,0:T(8,128)(2,1)} async-done(((bf16[4,256,576]{1,2,0:T(8,128)(2,1)}), bf16[4,256,576]{1,2,0:T(8,128)(2,1)}, u32[]{:S(2)}, u32[]{:S(2)}) %all-to-all-start) | async-done | bytes 1179680 | tf_op jit(solution)/shard_map/all_to_all | solution.py:174
  46.3 1.7 %copy.46.in_ref = bf16[4,256,576]{2,1,0:T(8,128)(2,1)S(1)} copy(bf16[4,256,576]{1,2,0:T(8,128)(2,1)} %all-to-all-done) | data formatting | bytes 2359296 | tf_op jit(solution)/shard_map/all_to_all | solution.py:174
  47.9 0.0 copy-done
  47.9 0.0 copy-done.2
  48.0 0.0 copy-start.1
  48.0 1.2 %copy-done.1 = f32[4,2,2,128,128]{4,3,2,1,0:T(8,128)S(1)} copy-done((f32[4,2,2,128,128]{4,3,2,1,0:T(8,128)S(1)}, f32[4,2,2,128,128]{4,3,2,1,0:T(8,128)}, u32[]{:S(2)}) %copy-start.1) | copy-done | bytes 1048600
  49.2 27.4 %merge_levels.1 = bf16[4,256,512]{2,1,0:T(8,128)(2,1)S(1)} custom-call(s32[1]{0:T(128)} %bitcast.start_ref, f32[4,4]{1,0:T(4,128)S(1)} %copy-done.2, s32[4,2,128,4]{3,2,1,0:T(8,128)S(1)} %pad_add_fusion.masks_ref, bf16[4,2,2,2,128,128]{5,4,3,2,1,0:T(8,128)(2,1)S(1)} %copy-done, f32[4,2,2,128,128]{4,3,2,1,0:T(8,128)S(1)} %copy-done.1, ...), custom_call_target="tpu_custom_call" | custom-call | tf_op jit(solution)/shard_map/merge_levels/pallas_call | solution.py:127
  76.6 28.6 %all_to_all.10 = bf16[4,256,512]{2,1,0:T(8,128)(2,1)S(1)} all-to-all(bf16[4,256,512]{2,1,0:T(8,128)(2,1)S(1)} %merge_levels.1), channel_id=1, replica_groups=mesh['img'=2,'sub'=4,'rng'=4] {'sub'}, dimensions={0} | all-to-all | bytes 2097152 | tf_op jit(solution)/shard_map/all_to_all | solution.py:179
  105.1 1.1 %copy.47 = bf16[2,2,128,2,512]{4,3,2,1,0:T(2,128)(2,1)S(1)} copy(bf16[2,2,128,2,512]{4,2,0,1,3:T(8,128)(2,1)S(1)} %bitcast.16) | data formatting | bytes 2097152 | tf_op jit(solution)/shard_map/transpose | solution.py:181
  106.2 1.5 %reshape.20 = bf16[2,2,128,1024]{3,2,1,0:T(8,128)(2,1)} reshape(bf16[2,2,128,2,512]{4,3,2,1,0:T(2,128)(2,1)S(1)} %copy.47) | data formatting | bytes 2097152 | tf_op jit(solution)/shard_map/reshape | solution.py:181
  (2 shorter events, 0.0 us)
Async XLA Ops:
  1.1 5.7 %collective-permute-start.1 = (bf16[2,2,128,32]{3,2,1,0:T(8,128)(2,1)S(1)}, bf16[2,2,128,32]{3,2,1,0:T(8,128)(2,1)S(1)}, u32[]{:S(2)}, u32[]{:S(2)}) collective-permute-start(bf16[2,2,128,32]{3,2,1,0:T(8,128)(2,1)S(1)} %get-tuple-element.10), channel_id=1, source_target_pairs={{1,0},{2,1},{3,2},{5,4},{6,5},{7,6},{9,8},{10,9},{11,10},{13,12},{... | collective-permute-start | bytes 98312 | tf_op jit(solution)/shard_map/ppermute | solution.py:147
  2.4 5.1 %collective-permute-start = (bf16[2,2,128,32]{3,2,1,0:T(8,128)(2,1)S(1)}, bf16[2,2,128,32]{3,2,1,0:T(8,128)(2,1)S(1)}, u32[]{:S(2)}, u32[]{:S(2)}) collective-permute-start(bf16[2,2,128,32]{3,2,1,0:T(8,128)(2,1)S(1)} %get-tuple-element.9), channel_id=1, source_target_pairs={{0,1},{1,2},{2,3},{4,5},{5,6},{6,7},{8,9},{9,10},{10,11},{12,13},{... | collective-permute-start | bytes 98312 | tf_op jit(solution)/shard_map/ppermute | solution.py:146
  6.8 1.2 %copy-start.3 = (bf16[2,2,128,1024]{3,2,1,0:T(8,128)(2,1)S(1)}, bf16[2,2,128,1024]{3,2,1,0:T(8,128)(2,1)}, u32[]{:S(2)}) copy-start(bf16[2,2,128,1024]{3,2,1,0:T(8,128)(2,1)} %param.5) | copy-start | bytes 3145732
  9.9 6.5 %copy-start.4 = (s32[4,2,128]{2,1,0:T(2,128)S(1)}, s32[4,2,128]{2,1,0:T(2,128)}, u32[]{:S(2)}) copy-start(s32[4,2,128]{2,1,0:T(2,128)} %param.8) | copy-start | bytes 12292
  9.9 36.4 %all-to-all-start = ((bf16[4,256,576]{1,2,0:T(8,128)(2,1)}), bf16[4,256,576]{1,2,0:T(8,128)(2,1)}, u32[]{:S(2)}, u32[]{:S(2)}) async-start(bf16[4,256,576]{1,2,0:T(8,128)(2,1)} %pad_maximum_fusion), calls=%async_computation | async-start | bytes 2359296 | tf_op jit(solution)/shard_map/all_to_all | solution.py:174
  17.8 30.2 %copy-start = (bf16[4,2,2,2,128,128]{5,4,3,2,1,0:T(8,128)(2,1)S(1)}, bf16[4,2,2,2,128,128]{5,4,3,2,1,0:T(8,128)(2,1)}, u32[]{:S(2)}) copy-start(bf16[4,2,2,2,128,128]{5,4,3,2,1,0:T(8,128)(2,1)} %weights_ref.1) | copy-start | bytes 3145732
  17.8 30.2 %copy-start.2 = (f32[4,4]{1,0:T(4,128)S(1)}, f32[4,4]{1,0:T(4,128)}, u32[]{:S(2)}) copy-start(f32[4,4]{1,0:T(4,128)} %taps_ref.1) | copy-start | bytes 196
  48.0 1.2 %copy-start.1 = (f32[4,2,2,128,128]{4,3,2,1,0:T(8,128)S(1)}, f32[4,2,2,128,128]{4,3,2,1,0:T(8,128)}, u32[]{:S(2)}) copy-start(f32[4,2,2,128,128]{4,3,2,1,0:T(8,128)} %constant.40.clone.table_ref) | copy-start | bytes 3145732

commit v2 on v1

--- a/solution.py
+++ b/solution.py
@@ -16,6 +16,7 @@
 LANES = 128
 PERIOD = 64
 ROWS = 32
+CHUNKS = 2
 
 
 def phases_of(bit_count):
@@ -47,21 +48,24 @@
     return jnp.stack(bits, axis=-1)
 
 
-def merge_kernel(start_ref, taps_ref, masks_ref, weights_ref, table_ref, in_ref, out_ref,
-                 x_ref, y_ref, w_ref, *, places, margin, total):
-    members, _, wide = x_ref.shape
-    given = in_ref.shape[-1]
-    width = out_ref.shape[-1]
-    start = start_ref[0]
+def merge_kernel(info_ref, taps_ref, masks_ref, weights_ref, table_ref, *refs, places, margin, total, members):
+    in_refs, out_refs = refs[:members], refs[members:2 * members]
+    x_ref, y_ref, w_ref = refs[2 * members:]
+    _, _, wide = x_ref.shape
+    given = in_refs[0].shape[-1]
+    width = out_refs[0].shape[-1]
+    start = info_ref[0]
     n_levels = len(places)
     x_ref[:, :, wide - LANES:] = jnp.zeros((members, 2 * ANGLES, LANES), jnp.bfloat16)
-    x_ref[:, :, 0:given] = in_ref[...]
+    for q in range(members):
+        x_ref[q, :, 0:given] = in_refs[q][...]
     for level in range(n_levels):
         place = places[level]
+        mine = (info_ref[1] >> place) & 1
         for h in range(2):
             for e in range(2):
-                real = weights_ref[level, e, h, 0]
-                imag = weights_ref[level, e, h, 1]
+                real = weights_ref[level, mine ^ e, mine ^ h, 0]
+                imag = weights_ref[level, mine ^ e, mine ^ h, 1]
                 r0, c0 = h * 2 * ANGLES, e * 2 * ANGLES
                 w_ref[r0:r0 + ANGLES, c0:c0 + ANGLES] = real
                 w_ref[r0:r0 + ANGLES, c0 + ANGLES:c0 + 2 * ANGLES] = -imag
@@ -72,8 +76,8 @@
         for side in range(2):
             own = [p for p in range(members) if (p >> place) % 2 == side]
 
-            def rows_step(block, carry, side=side, own=own, level=level, taps=taps):
-                flags = masks_ref[level, side, pl.ds(pl.multiple_of(block * ROWS, ROWS), ROWS), :]
+            def rows_step(block, carry, side=side, own=own, level=level, taps=taps, mine=mine):
+                flags = masks_ref[level, mine ^ side, pl.ds(pl.multiple_of(block * ROWS, ROWS), ROWS), :]
                 masks = [jnp.broadcast_to(flags[:, k:k + 1], (ROWS, wide)) != 0 for k in range(4)]
                 for p in own:
                     for c in range(2):
@@ -99,8 +103,8 @@
                 z = jnp.dot(w_ref[r0:r0 + 2 * ANGLES, 0:2 * ANGLES], y_ref[low], preferred_element_type=jnp.float32)
                 z = z + jnp.dot(w_ref[r0:r0 + 2 * ANGLES, 2 * ANGLES:], y_ref[high], preferred_element_type=jnp.float32)
                 dest = high if h else low
-                cosine = table_ref[level, 0, h]
-                sinus = table_ref[level, 1, h]
+                cosine = table_ref[level, 0, mine ^ h]
+                sinus = table_ref[level, 1, mine ^ h]
                 for tile in range(wide // LANES):
                     at = tile * LANES
                     zr = z[:ANGLES, at:at + LANES]
@@ -115,28 +119,29 @@
                     x_ref[dest, ANGLES:, at:at + LANES] = im.astype(jnp.bfloat16)
     for p in range(members):
         v = x_ref[p].astype(jnp.float32)
-        out_ref[p] = pltpu.roll(v, wide - margin, 1)[:, :width].astype(jnp.bfloat16)
-
-
-def merge_levels(start, taps, masks, weights, table, pieces, places, margin, total):
-    members, rows, given = pieces.shape
+        out_refs[p][...] = pltpu.roll(v, wide - margin, 1)[:, :width].astype(jnp.bfloat16)
+
+
+def merge_levels(info, taps, masks, weights, table, pieces, places, margin, total):
+    members = len(pieces)
+    rows, given = pieces[0].shape
     width = given - 2 * margin
     wide = -(-given // LANES) * LANES
     smem = pl.BlockSpec(memory_space=pltpu.SMEM)
     vmem = pl.BlockSpec(memory_space=pltpu.VMEM)
     return pl.pallas_call(
-        functools.partial(merge_kernel, places=places, margin=margin, total=total),
-        out_shape=jax.ShapeDtypeStruct((members, rows, width), jnp.bfloat16),
-        in_specs=[smem, smem, vmem, vmem, vmem, vmem],
-        out_specs=vmem,
+        functools.partial(merge_kernel, places=places, margin=margin, total=total, members=members),
+        out_shape=[jax.ShapeDtypeStruct((rows, width), jnp.bfloat16)] * members,
+        in_specs=[smem, smem] + [vmem] * (3 + members),
+        out_specs=[vmem] * members,
         scratch_shapes=[
             pltpu.VMEM((members, rows, wide), jnp.bfloat16),
             pltpu.VMEM((members, rows, wide), jnp.bfloat16),
             pltpu.VMEM((4 * ANGLES, 4 * ANGLES), jnp.bfloat16),
         ],
-        compiler_params=pltpu.CompilerParams(vmem_limit_bytes=48 * 2**20),
+        compiler_params=pltpu.CompilerParams(vmem_limit_bytes=32 * 2**20),
         name="merge_levels",
-    )(start, taps, masks, weights, table, pieces)
+    )(info, taps, masks, weights, table, *pieces)
 
 
 def with_halo(cells, axis, margin):
@@ -146,6 +151,21 @@
     left = lax.ppermute(tail, axis, [(i, i + 1) for i in range(count - 1)])
     right = lax.ppermute(head, axis, [(i + 1, i) for i in range(count - 1)])
     return jnp.concatenate([left, cells, right], axis=-1)
+
+
+def pick(items, q, member):
+    def chosen(j, slot):
+        if j < 0:
+            return items[slot]
+        return jnp.where((member >> j) & 1 == 1, chosen(j - 1, slot ^ (1 << j)), chosen(j - 1, slot))
+    return chosen(len(items).bit_length() - 2, q)
+
+
+def swap(value, q, distinct, sub_count):
+    if q == 0:
+        return value
+    mask = sum(((q >> j) & 1) << bit for j, bit in enumerate(distinct))
+    return lax.ppermute(value, "sub", [(i, i ^ mask) for i in range(sub_count)])
 
 
 def on_device(image, interp_weights, range_taps, range_shifts):
@@ -159,26 +179,36 @@
         members = 2 ** len(distinct)
         parts = members // groups
         width = range_width // parts
+        step = width // CHUNKS
         margin = len(levels) * RIM
         first, end = levels[0], levels[-1] + 1
-        spread = [sum(((p >> j) & 1) << bit for j, bit in enumerate(distinct)) for p in range(members)]
-        bases = [i for i in range(sub_count) if all(not (i >> bit) & 1 for bit in distinct)]
-        index_groups = None if len(bases) == 1 else [[base + s for s in spread] for base in bases]
         member = sum(((sub_index >> bit) & 1) << j for j, bit in enumerate(distinct))
-        start = lax.axis_index("rng") * range_width + member // groups * width - margin
+        start = lax.axis_index("rng") * range_width + (member >> (groups.bit_length() - 1)) * width - margin
         padded = with_halo(current, "rng", margin)
-        pieces = jnp.stack([
-            padded[:, p % groups, :, p // groups * width:p // groups * width + width + 2 * margin]
-            for p in range(members)
-        ]).reshape(members, 2 * ANGLES, width + 2 * margin)
-        pieces = lax.all_to_all(pieces, "sub", 0, 0, axis_index_groups=index_groups, tiled=True)
-        merged = merge_levels(
-            start.reshape(1).astype(jnp.int32), range_taps[first:end], masks[first:end],
-            interp_weights[first:end], jnp.asarray(phase_table(levels, margin)), pieces,
-            [distinct.index(bit) for bit in bits], margin, total)
-        back = lax.all_to_all(merged, "sub", 0, 0, axis_index_groups=index_groups, tiled=True)
-        back = back.reshape(parts, groups, 2, ANGLES, width)
-        current = jnp.transpose(back, (2, 1, 3, 0, 4)).reshape(image.shape)
+        table = jnp.asarray(phase_table(levels, margin))
+        columns = [[None] * CHUNKS for _ in range(members)]
+        pieces = []
+        for chunk in range(CHUNKS):
+            windows = []
+            for p in range(members):
+                at = p // groups * width + chunk * step
+                windows.append(padded[:, p % groups, :, at:at + step + 2 * margin])
+            pieces.append([
+                swap(pick(windows, q, member).reshape(2 * ANGLES, step + 2 * margin), q, distinct, sub_count)
+                for q in range(members)
+            ])
+        for chunk in range(CHUNKS):
+            info = jnp.stack([start + chunk * step, member]).astype(jnp.int32)
+            merged = merge_levels(
+                info, range_taps[first:end], masks[first:end], interp_weights[first:end], table,
+                pieces[chunk], [distinct.index(bit) for bit in bits], margin, total)
+            back = [swap(merged[q], q, distinct, sub_count) for q in range(members)]
+            for p in range(members):
+                columns[p][chunk] = pick(back, p, member).reshape(2, ANGLES, step)
+        current = jnp.stack([
+            jnp.concatenate([columns[part * groups + m][chunk] for part in range(parts) for chunk in range(CHUNKS)], axis=-1)
+            for m in range(groups)
+        ], axis=1)
     return current
 
 

time: 108 us -> 106 us (0.981)
  blocking collectives: 28.6 us -> 0 us
  starting transfers between devices: 10.8 us -> 35.4 us
  waiting for transfers between devices: 28.5 us -> 12.2 us
  Pallas kernels: 27.4 us -> 41.6 us
  other arithmetic: 1.99 us -> 9.41 us
  local copies, waits for them, and re-layouts: 10.4 us -> 7.07 us
    ppermute x0 -> x12, starting transfers between devices: none -> 30.4 us  [swap(): return lax.ppermute(value, 'sub', [(i, i ^ mask) for i in range(sub_count)])]
    all_to_all x1 -> x0, blocking collectives: 28.6 us -> none  [on_device(): lax.all_to_all(merged, 'sub', 0, 0, axis_index_groups=index_groups, tiled...]
    all_to_all x1 -> x0, waiting for transfers between devices: 28.4 us -> none  [on_device(): lax.all_to_all(pieces, 'sub', 0, 0, axis_index_groups=index_groups, tiled...]
    pallas_call x1 -> x2, Pallas kernels: 27.4 us -> 41.6 us  [merge_levels(): pl.pallas_call(functools.partial(merge_kernel, places=places, margin=marg...]
    ppermute x0 -> x12, waiting for transfers between devices: none -> 12.2 us  [swap(): return lax.ppermute(value, 'sub', [(i, i ^ mask) for i in range(sub_count)])]
    all_to_all x1 -> x0, starting transfers between devices: 6.48 us -> none  [on_device(): lax.all_to_all(pieces, 'sub', 0, 0, axis_index_groups=index_groups, tiled...]
    select_n x0 -> x4, other arithmetic: none -> 6.47 us  [chosen(): jnp.where(member >> j & 1 == 1, chosen(j - 1, slot ^ 1 << j), chosen(j -...]
    all_to_all x1 -> x0, local copies, waits for them, and re-layouts: 1.68 us -> none  [on_device(): lax.all_to_all(pieces, 'sub', 0, 0, axis_index_groups=index_groups, tiled...]
  transfers between devices with their start and end apart: 3 -> 14, of which waited for: 1 -> 3; matrix products, arithmetic and copies ran while one was open for 3% -> 11% of each run, Pallas kernels for 0% -> 39%
where the time goes in v2:
time: 106 us
  Pallas kernels  41.6 us (39%)
  starting transfers between devices  35.4 us (33%)
  waiting for transfers between devices  12.2 us (12%)
  other arithmetic  9.41 us (9%)
  local copies, waits for them, and re-layouts  7.07 us (7%)
    pallas_call x2, Pallas kernels, merge_levels(): pl.pallas_call(functools.partial(merge_kernel, places=places, margin=marg...  41.6 us
    ppermute x12, starting transfers between devices, swap(): return lax.ppermute(value, 'sub', [(i, i ^ mask) for i in range(sub_count)])  30.4 us
    ppermute x12, waiting for transfers between devices, swap(): return lax.ppermute(value, 'sub', [(i, i ^ mask) for i in range(sub_count)])  12.2 us
    select_n x4, other arithmetic, chosen(): jnp.where(member >> j & 1 == 1, chosen(j - 1, slot ^ 1 << j), chosen(j -...  6.47 us
    ppermute x1, starting transfers between devices, with_halo(): left = lax.ppermute(tail, axis, [(i, i + 1) for i in range(count - 1)])  3.69 us
    unnamed x15, local copies, waits for them, and re-layouts  3.61 us
  transfers between devices with their start and end apart: 14, of which 3 were waited for; matrix products, arithmetic and copies ran while one was open for 11% of the time, Pallas kernels for 39%

profile of v2, /device:TPU:0, one launch (start us, length us, event | category | flops | bytes accessed | tf_op | source)
XLA Modules:
  0.0 105.7 jit_solution(17520779474207432407)
XLA Ops:
  0.0 1.1 %fusion = (bf16[2,2,128,32]{3,2,1,0:T(8,128)(2,1)S(1)}, bf16[2,2,128,32]{3,2,1,0:T(8,128)(2,1)S(1)}) fusion(bf16[2,2,128,1024]{3,2,1,0:T(8,128)(2,1)} %param.5), kind=kLoop, calls=%fused_computation.47 | loop fusion | bytes 131072 | tf_op jit(solution)/shard_map/slice | solution.py:150
  1.1 0.0 copy-start.6
  1.1 1.3 %collective-permute-start.7 = (bf16[2,2,128,32]{3,2,1,0:T(8,128)(2,1)S(1)}, bf16[2,2,128,32]{3,2,1,0:T(8,128)(2,1)S(1)}, u32[]{:S(2)}, u32[]{:S(2)}) collective-permute-start(bf16[2,2,128,32]{3,2,1,0:T(8,128)(2,1)S(1)} %get-tuple-element.32), channel_id=1, source_target_pairs={{1,0},{2,1},{3,2},{5,4},{6,5},{7,6},{9,8},{10,9},{11,10},{13,12},{... | collective-permute-start | bytes 98312 | tf_op jit(solution)/shard_map/ppermute | solution.py:152
  2.4 3.7 %collective-permute-start = (bf16[2,2,128,32]{3,2,1,0:T(8,128)(2,1)S(1)}, bf16[2,2,128,32]{3,2,1,0:T(8,128)(2,1)}, u32[]{:S(2)}, u32[]{:S(2)}) collective-permute-start(bf16[2,2,128,32]{3,2,1,0:T(8,128)(2,1)S(1)} %get-tuple-element.31), channel_id=1, source_target_pairs={{0,1},{1,2},{2,3},{4,5},{5,6},{6,7},{8,9},{9,10},{10,11},{12,13},{... | collective-permute-start | bytes 98312 | tf_op jit(solution)/shard_map/ppermute | solution.py:151
  6.1 2.3 %constant_dynamic-update-slice_fusion.1 = bf16[2,2,128,1056]{3,2,1,0:T(8,128)(2,1)} fusion(bf16[2,2,128,1024]{3,2,1,0:T(8,128)(2,1)} %param.5), kind=kLoop, calls=%fused_computation.39 | loop fusion | bytes 2097152
  8.4 0.0 copy-done.6
  8.4 0.2 copy.31
  8.6 0.2 copy.30
  8.9 0.2 copy.29
  9.1 1.0 copy.28
  10.1 0.0 copy-start.5
  10.1 1.6 %pad_add_fusion.masks_ref = s32[4,2,128,4]{3,2,1,0:T(8,128)S(1)} fusion(s32[4,2,128,1]{3,2,1,0:T(8,128)S(1)} %copy.31, s32[4,2,128,1]{3,2,1,0:T(8,128)S(1)} %copy.30, s32[4,2,128,1]{3,2,1,0:T(8,128)S(1)} %copy.29, s32[4,2,128,1]{3,2,1,0:T(8,128)} %copy.28), kind=kLoop, calls=%fused_computation.1 | loop fusion | flops 12288 | bytes 32768 | tf_op jit(solution)/shard_map/stack | solution.py:48
  11.7 0.0 collective-permute-done.7
  11.8 0.7 constant_dynamic-update-slice_fusion
  12.4 0.0 copy-done.5
  12.4 1.4 %broadcast_select_fusion.8 = (bf16[2,1,128,320]{3,2,1,0:T(8,128)(2,1)S(1)}, bf16[2,1,128,320]{3,2,1,0:T(8,128)(2,1)S(1)}, bf16[2,1,128,320]{3,2,1,0:T(8,128)(2,1)S(1)}, bf16[2,1,128,320]{3,2,1,0:T(8,128)(2,1)S(1)}) fusion(pred[]{:T(512)S(6)} %eq.4, bf16[2,2,128,1056]{3,2,1,0:T(8,128)(2,1)} %constant_dynamic-update-slice_fusion, pred[]{:T(512)S(6)} %eq.5, ...), kind=kLoop, calls=%fused_computation.14 | loop fusion | flops 655360 | bytes 1310722 | tf_op jit(solution)/shard_map/jit(_where)/select_n | solution.py:160
  13.8 3.1 %collective-permute-start.8 = (bf16[256,320]{1,0:T(8,128)(2,1)S(1)}, bf16[256,320]{1,0:T(8,128)(2,1)S(1)}, u32[]{:S(2)}, u32[]{:S(2)}) collective-permute-start(bf16[256,320]{1,0:T(8,128)(2,1)S(1)} %bitcast.43), channel_id=1, source_target_pairs={{0,4},{4,0},{8,12},{12,8},{1,5},{5,1},{9,13},{13,9},{2,6},{6,2},{1... | collective-permute-start | bytes 491528 | tf_op jit(solution)/shard_map/ppermute | solution.py:168
  16.9 2.6 %collective-permute-start.9 = (bf16[256,320]{1,0:T(8,128)(2,1)S(1)}, bf16[256,320]{1,0:T(8,128)(2,1)S(1)}, u32[]{:S(2)}, u32[]{:S(2)}) collective-permute-start(bf16[256,320]{1,0:T(8,128)(2,1)S(1)} %bitcast.42), channel_id=1, source_target_pairs={{0,8},{4,12},{8,0},{12,4},{1,9},{5,13},{9,1},{13,5},{2,10},{6,14},... | collective-permute-start | bytes 491528 | tf_op jit(solution)/shard_map/ppermute | solution.py:168
  19.5 0.0 collective-permute-start.10
  19.5 0.0 collective-permute-done
  19.5 0.0 copy-start.1
  19.5 2.0 %broadcast_select_fusion.12 = (bf16[2,1,128,320]{3,2,1,0:T(8,128)(2,1)}, bf16[2,1,128,320]{3,2,1,0:T(8,128)(2,1)S(1)}, bf16[2,1,128,320]{3,2,1,0:T(8,128)(2,1)S(1)}) fusion(pred[]{:T(512)S(6)} %eq.4, pred[]{:T(512)S(6)} %eq.5, bf16[2,2,128,1024]{3,2,1,0:T(8,128)(2,1)S(1)} %copy-done.5, bf16[2,2,128,32]{3,2,1,0:T(8,128)(2,1)} %collective-permute-done), kind=kLoop, calls=%fused_computation.18 | loop fusion | flops 901120 | bytes 1966082 | tf_op jit(solution)/shard_map/jit(_where)/select_n | solution.py:160
  21.6 0.0 copy-start
  21.6 0.0 copy-start.2
  21.6 2.1 %broadcast_select_fusion.13 = (bf16[2,1,128,320]{3,2,1,0:T(8,128)(2,1)}, bf16[2,1,128,320]{3,2,1,0:T(8,128)(2,1)}, bf16[2,1,128,320]{3,2,1,0:T(8,128)(2,1)S(1)}) fusion(pred[]{:T(512)S(6)} %eq.4, bf16[2,1,128,320]{3,2,1,0:T(8,128)(2,1)S(1)} %get-tuple-element.23, bf16[2,1,128,320]{3,2,1,0:T(8,128)(2,1)S(1)} %get-tuple-element.22, pred[]{:T(512)S(6)} %eq.5, ...), kind=kLoop, calls=%fused_computation.19 | loop fusion | flops 573440 | bytes 1146882 | tf_op jit(solution)/shard_map/jit(_where)/select_n | solution.py:160
  23.6 0.9 collective-permute-start.1
  24.5 3.5 %collective-permute-start.2 = (bf16[256,320]{1,0:T(8,128)(2,1)}, bf16[256,320]{1,0:T(8,128)(2,1)S(1)}, u32[]{:S(2)}, u32[]{:S(2)}) collective-permute-start(bf16[256,320]{1,0:T(8,128)(2,1)} %bitcast.8), channel_id=1, source_target_pairs={{0,8},{4,12},{8,0},{12,4},{1,9},{5,13},{9,1},{13,5},{2,10},{6,14},... | collective-permute-start | bytes 491528 | tf_op jit(solution)/shard_map/ppermute | solution.py:168
  28.0 0.0 collective-permute-done.8.refs_1_
  28.0 1.2 %collective-permute-start.3 = (bf16[256,320]{1,0:T(8,128)(2,1)}, bf16[256,320]{1,0:T(8,128)(2,1)S(1)}, u32[]{:S(2)}, u32[]{:S(2)}) collective-permute-start(bf16[256,320]{1,0:T(8,128)(2,1)} %bitcast.9), channel_id=1, source_target_pairs={{0,12},{4,8},{8,4},{12,0},{1,13},{5,9},{9,5},{13,1},{2,14},{6,10},... | collective-permute-start | bytes 491528 | tf_op jit(solution)/shard_map/ppermute | solution.py:168
  29.2 0.1 pad_add_fusion.2.info_ref
  29.3 4.8 %collective-permute-done.9.refs_2_ = bf16[256,320]{1,0:T(8,128)(2,1)S(1)} collective-permute-done((bf16[256,320]{1,0:T(8,128)(2,1)S(1)}, bf16[256,320]{1,0:T(8,128)(2,1)S(1)}, u32[]{:S(2)}, u32[]{:S(2)}) %collective-permute-start.9) | collective-permute-done | bytes 163872 | tf_op jit(solution)/shard_map/ppermute | solution.py:168
  34.1 0.0 collective-permute-done.10.refs_3_
  34.1 0.0 copy-done.1
  34.1 0.0 copy-done
  34.1 0.0 copy-done.2
  34.1 21.2 %merge_levels.3 = (bf16[256,256]{1,0:T(8,128)(2,1)S(1)}, bf16[256,256]{1,0:T(8,128)(2,1)S(1)}, bf16[256,256]{1,0:T(8,128)(2,1)S(1)}, bf16[256,256]{1,0:T(8,128)(2,1)}) custom-call(s32[2]{0:T(128)S(1)} %pad_add_fusion.2.info_ref, f32[4,4]{1,0:T(4,128)S(1)} %copy-done.2, s32[4,2,128,4]{3,2,1,0:T(8,128)S(1)} %pad_add_fusion.masks_ref, ...), custom_call_target="tpu_custom_call" | custom-call | tf_op jit(solution)/shard_map/merge_levels/pallas_call | solution.py:132
  55.3 0.0 copy-start.3
  55.3 0.6 copy-done.3
  56.0 0.0 copy-start.4
  56.0 0.6 copy-done.4
  56.6 2.5 %collective-permute-start.11 = (bf16[256,256]{1,0:T(8,128)(2,1)}, bf16[256,256]{1,0:T(8,128)(2,1)}, u32[]{:S(2)}, u32[]{:S(2)}) collective-permute-start(bf16[256,256]{1,0:T(8,128)(2,1)} %get-tuple-element.17), channel_id=1, source_target_pairs={{0,12},{4,8},{8,4},{12,0},{1,13},{5,9},{9,5},{13,1},{2,14},{6,10},... | collective-permute-start | bytes 393224 | tf_op jit(solution)/shard_map/ppermute | solution.py:168
  59.1 0.1 pad_add_fusion.1.info_ref
  59.2 12.2 %collective-permute-start.12 = (bf16[256,256]{1,0:T(8,128)(2,1)}, bf16[256,256]{1,0:T(8,128)(2,1)S(1)}, u32[]{:S(2)}, u32[]{:S(2)}) collective-permute-start(bf16[256,256]{1,0:T(8,128)(2,1)} %copy-done.4), channel_id=1, source_target_pairs={{0,8},{4,12},{8,0},{12,4},{1,9},{5,13},{9,1},{13,5},{2,10},{6,14},... | collective-permute-start | bytes 393224 | tf_op jit(solution)/shard_map/ppermute | solution.py:168
  71.4 0.0 collective-permute-done.1.refs_1_
  71.4 0.2 collective-permute-start.13
  71.6 0.0 collective-permute-done.2.refs_2_
  71.6 0.0 collective-permute-done.3.refs_3_
  71.6 20.4 %merge_levels.2 = (bf16[256,256]{1,0:T(8,128)(2,1)S(1)}, bf16[256,256]{1,0:T(8,128)(2,1)S(1)}, bf16[256,256]{1,0:T(8,128)(2,1)S(1)}, bf16[256,256]{1,0:T(8,128)(2,1)S(1)}) custom-call(s32[2]{0:T(128)S(1)} %pad_add_fusion.1.info_ref, f32[4,4]{1,0:T(4,128)S(1)} %copy-done.2, s32[4,2,128,4]{3,2,1,0:T(8,128)S(1)} %pad_add_fusion.masks_ref, ...), custom_call_target="tpu_custom_call" | custom-call | tf_op jit(solution)/shard_map/merge_levels/pallas_call | solution.py:132
  91.9 2.9 %collective-permute-start.5 = (bf16[256,256]{1,0:T(8,128)(2,1)S(1)}, bf16[256,256]{1,0:T(8,128)(2,1)S(1)}, u32[]{:S(2)}, u32[]{:S(2)}) collective-permute-start(bf16[256,256]{1,0:T(8,128)(2,1)S(1)} %get-tuple-element.14), channel_id=1, source_target_pairs={{0,8},{4,12},{8,0},{12,4},{1,9},{5,13},{9,1},{13,5},{2,10},{6,14},... | collective-permute-start | bytes 393224 | tf_op jit(solution)/shard_map/ppermute | solution.py:168
  94.8 1.3 %collective-permute-start.4 = (bf16[256,256]{1,0:T(8,128)(2,1)S(1)}, bf16[256,256]{1,0:T(8,128)(2,1)S(1)}, u32[]{:S(2)}, u32[]{:S(2)}) collective-permute-start(bf16[256,256]{1,0:T(8,128)(2,1)S(1)} %get-tuple-element.13), channel_id=1, source_target_pairs={{0,12},{4,8},{8,4},{12,0},{1,13},{5,9},{9,5},{13,1},{2,14},{6,10},... | collective-permute-start | bytes 393224 | tf_op jit(solution)/shard_map/ppermute | solution.py:168
  96.2 0.0 collective-permute-done.11
  96.2 0.0 collective-permute-start.6
  96.2 0.0 collective-permute-done.12
  96.2 0.0 collective-permute-done.13
  96.2 7.1 %collective-permute-done.5 = bf16[256,256]{1,0:T(8,128)(2,1)S(1)} collective-permute-done((bf16[256,256]{1,0:T(8,128)(2,1)S(1)}, bf16[256,256]{1,0:T(8,128)(2,1)S(1)}, u32[]{:S(2)}, u32[]{:S(2)}) %collective-permute-start.5) | collective-permute-done | bytes 131104 | tf_op jit(solution)/shard_map/ppermute | solution.py:168
  103.3 0.0 collective-permute-done.4
  103.3 0.2 collective-permute-done.6
  103.5 1.0 broadcast_select_fusion.30
  104.5 0.1 maximum_bitcast_fusion.1
  104.6 0.1 maximum_bitcast_fusion
  104.7 1.1 %pad_maximum_fusion = bf16[2,2,128,1024]{3,2,1,0:T(8,128)(2,1)} fusion(bf16[2,1,128,1024]{3,2,1,0:T(8,128)(2,1)S(1)} %maximum_bitcast_fusion.1, bf16[2,1,128,1024]{3,2,1,0:T(8,128)(2,1)S(1)} %maximum_bitcast_fusion), kind=kLoop, calls=%fused_computation | loop fusion | flops 524288 | bytes 2097152 | tf_op jit(solution)/shard_map/stack | solution.py:208
  (1 shorter events, 0.0 us)
Async XLA Ops:
  1.1 7.3 %copy-start.6 = (s32[4,2,128]{2,1,0:T(2,128)S(1)}, s32[4,2,128]{2,1,0:T(2,128)}, u32[]{:S(2)}) copy-start(s32[4,2,128]{2,1,0:T(2,128)} %param.8) | copy-start | bytes 12292
  1.1 10.7 %collective-permute-start.7 = (bf16[2,2,128,32]{3,2,1,0:T(8,128)(2,1)S(1)}, bf16[2,2,128,32]{3,2,1,0:T(8,128)(2,1)S(1)}, u32[]{:S(2)}, u32[]{:S(2)}) collective-permute-start(bf16[2,2,128,32]{3,2,1,0:T(8,128)(2,1)S(1)} %get-tuple-element.32), channel_id=1, source_target_pairs={{1,0},{2,1},{3,2},{5,4},{6,5},{7,6},{9,8},{10,9},{11,10},{13,12},{... | collective-permute-start | bytes 98312 | tf_op jit(solution)/shard_map/ppermute | solution.py:152
  2.4 17.1 %collective-permute-start = (bf16[2,2,128,32]{3,2,1,0:T(8,128)(2,1)S(1)}, bf16[2,2,128,32]{3,2,1,0:T(8,128)(2,1)}, u32[]{:S(2)}, u32[]{:S(2)}) collective-permute-start(bf16[2,2,128,32]{3,2,1,0:T(8,128)(2,1)S(1)} %get-tuple-element.31), channel_id=1, source_target_pairs={{0,1},{1,2},{2,3},{4,5},{5,6},{6,7},{8,9},{9,10},{10,11},{12,13},{... | collective-permute-start | bytes 98312 | tf_op jit(solution)/shard_map/ppermute | solution.py:151
  10.1 2.3 %copy-start.5 = (bf16[2,2,128,1024]{3,2,1,0:T(8,128)(2,1)S(1)}, bf16[2,2,128,1024]{3,2,1,0:T(8,128)(2,1)}, u32[]{:S(2)}) copy-start(bf16[2,2,128,1024]{3,2,1,0:T(8,128)(2,1)} %param.5) | copy-start | bytes 3145732
  13.8 14.2 %collective-permute-start.8 = (bf16[256,320]{1,0:T(8,128)(2,1)S(1)}, bf16[256,320]{1,0:T(8,128)(2,1)S(1)}, u32[]{:S(2)}, u32[]{:S(2)}) collective-permute-start(bf16[256,320]{1,0:T(8,128)(2,1)S(1)} %bitcast.43), channel_id=1, source_target_pairs={{0,4},{4,0},{8,12},{12,8},{1,5},{5,1},{9,13},{13,9},{2,6},{6,2},{1... | collective-permute-start | bytes 491528 | tf_op jit(solution)/shard_map/ppermute | solution.py:168
  16.9 17.2 %collective-permute-start.9 = (bf16[256,320]{1,0:T(8,128)(2,1)S(1)}, bf16[256,320]{1,0:T(8,128)(2,1)S(1)}, u32[]{:S(2)}, u32[]{:S(2)}) collective-permute-start(bf16[256,320]{1,0:T(8,128)(2,1)S(1)} %bitcast.42), channel_id=1, source_target_pairs={{0,8},{4,12},{8,0},{12,4},{1,9},{5,13},{9,1},{13,5},{2,10},{6,14},... | collective-permute-start | bytes 491528 | tf_op jit(solution)/shard_map/ppermute | solution.py:168
  19.5 14.6 %collective-permute-start.10 = (bf16[256,320]{1,0:T(8,128)(2,1)S(1)}, bf16[256,320]{1,0:T(8,128)(2,1)S(1)}, u32[]{:S(2)}, u32[]{:S(2)}) collective-permute-start(bf16[256,320]{1,0:T(8,128)(2,1)S(1)} %bitcast.41), channel_id=1, source_target_pairs={{0,12},{4,8},{8,4},{12,0},{1,13},{5,9},{9,5},{13,1},{2,14},{6,10},... | collective-permute-start | bytes 491528 | tf_op jit(solution)/shard_map/ppermute | solution.py:168
  19.5 14.6 %copy-start.1 = (f32[4,2,2,128,128]{4,3,2,1,0:T(8,128)S(1)}, f32[4,2,2,128,128]{4,3,2,1,0:T(8,128)}, u32[]{:S(2)}) copy-start(f32[4,2,2,128,128]{4,3,2,1,0:T(8,128)} %constant.31.clone.table_ref) | copy-start | bytes 3145732
  21.6 12.6 %copy-start = (bf16[4,2,2,2,128,128]{5,4,3,2,1,0:T(8,128)(2,1)S(1)}, bf16[4,2,2,2,128,128]{5,4,3,2,1,0:T(8,128)(2,1)}, u32[]{:S(2)}) copy-start(bf16[4,2,2,2,128,128]{5,4,3,2,1,0:T(8,128)(2,1)} %weights_ref.3) | copy-start | bytes 3145732
  21.6 12.6 %copy-start.2 = (f32[4,4]{1,0:T(4,128)S(1)}, f32[4,4]{1,0:T(4,128)}, u32[]{:S(2)}) copy-start(f32[4,4]{1,0:T(4,128)} %taps_ref.3) | copy-start | bytes 196
  23.6 47.7 %collective-permute-start.1 = (bf16[256,320]{1,0:T(8,128)(2,1)}, bf16[256,320]{1,0:T(8,128)(2,1)S(1)}, u32[]{:S(2)}, u32[]{:S(2)}) collective-permute-start(bf16[256,320]{1,0:T(8,128)(2,1)} %bitcast.7), channel_id=1, source_target_pairs={{0,4},{4,0},{8,12},{12,8},{1,5},{5,1},{9,13},{13,9},{2,6},{6,2},{1... | collective-permute-start | bytes 491528 | tf_op jit(solution)/shard_map/ppermute | solution.py:168
  24.5 47.0 %collective-permute-start.2 = (bf16[256,320]{1,0:T(8,128)(2,1)}, bf16[256,320]{1,0:T(8,128)(2,1)S(1)}, u32[]{:S(2)}, u32[]{:S(2)}) collective-permute-start(bf16[256,320]{1,0:T(8,128)(2,1)} %bitcast.8), channel_id=1, source_target_pairs={{0,8},{4,12},{8,0},{12,4},{1,9},{5,13},{9,1},{13,5},{2,10},{6,14},... | collective-permute-start | bytes 491528 | tf_op jit(solution)/shard_map/ppermute | solution.py:168
  28.0 43.5 %collective-permute-start.3 = (bf16[256,320]{1,0:T(8,128)(2,1)}, bf16[256,320]{1,0:T(8,128)(2,1)S(1)}, u32[]{:S(2)}, u32[]{:S(2)}) collective-permute-start(bf16[256,320]{1,0:T(8,128)(2,1)} %bitcast.9), channel_id=1, source_target_pairs={{0,12},{4,8},{8,4},{12,0},{1,13},{5,9},{9,5},{13,1},{2,14},{6,10},... | collective-permute-start | bytes 491528 | tf_op jit(solution)/shard_map/ppermute | solution.py:168
  55.3 0.6 copy-start.3
  56.0 0.6 copy-start.4
  56.6 39.6 %collective-permute-start.11 = (bf16[256,256]{1,0:T(8,128)(2,1)}, bf16[256,256]{1,0:T(8,128)(2,1)}, u32[]{:S(2)}, u32[]{:S(2)}) collective-permute-start(bf16[256,256]{1,0:T(8,128)(2,1)} %get-tuple-element.17), channel_id=1, source_target_pairs={{0,12},{4,8},{8,4},{12,0},{1,13},{5,9},{9,5},{13,1},{2,14},{6,10},... | collective-permute-start | bytes 393224 | tf_op jit(solution)/shard_map/ppermute | solution.py:168
  59.2 37.0 %collective-permute-start.12 = (bf16[256,256]{1,0:T(8,128)(2,1)}, bf16[256,256]{1,0:T(8,128)(2,1)S(1)}, u32[]{:S(2)}, u32[]{:S(2)}) collective-permute-start(bf16[256,256]{1,0:T(8,128)(2,1)} %copy-done.4), channel_id=1, source_target_pairs={{0,8},{4,12},{8,0},{12,4},{1,9},{5,13},{9,1},{13,5},{2,10},{6,14},... | collective-permute-start | bytes 393224 | tf_op jit(solution)/shard_map/ppermute | solution.py:168
  71.4 24.8 %collective-permute-start.13 = (bf16[256,256]{1,0:T(8,128)(2,1)}, bf16[256,256]{1,0:T(8,128)(2,1)S(1)}, u32[]{:S(2)}, u32[]{:S(2)}) collective-permute-start(bf16[256,256]{1,0:T(8,128)(2,1)} %copy-done.3), channel_id=1, source_target_pairs={{0,4},{4,0},{8,12},{12,8},{1,5},{5,1},{9,13},{13,9},{2,6},{6,2},{1... | collective-permute-start | bytes 393224 | tf_op jit(solution)/shard_map/ppermute | solution.py:168
  91.9 11.4 %collective-permute-start.5 = (bf16[256,256]{1,0:T(8,128)(2,1)S(1)}, bf16[256,256]{1,0:T(8,128)(2,1)S(1)}, u32[]{:S(2)}, u32[]{:S(2)}) collective-permute-start(bf16[256,256]{1,0:T(8,128)(2,1)S(1)} %get-tuple-element.14), channel_id=1, source_target_pairs={{0,8},{4,12},{8,0},{12,4},{1,9},{5,13},{9,1},{13,5},{2,10},{6,14},... | collective-permute-start | bytes 393224 | tf_op jit(solution)/shard_map/ppermute | solution.py:168
  94.8 8.5 %collective-permute-start.4 = (bf16[256,256]{1,0:T(8,128)(2,1)S(1)}, bf16[256,256]{1,0:T(8,128)(2,1)S(1)}, u32[]{:S(2)}, u32[]{:S(2)}) collective-permute-start(bf16[256,256]{1,0:T(8,128)(2,1)S(1)} %get-tuple-element.13), channel_id=1, source_target_pairs={{0,12},{4,8},{8,4},{12,0},{1,13},{5,9},{9,5},{13,1},{2,14},{6,10},... | collective-permute-start | bytes 393224 | tf_op jit(solution)/shard_map/ppermute | solution.py:168
  96.2 7.3 %collective-permute-start.6 = (bf16[256,256]{1,0:T(8,128)(2,1)S(1)}, bf16[256,256]{1,0:T(8,128)(2,1)S(1)}, u32[]{:S(2)}, u32[]{:S(2)}) collective-permute-start(bf16[256,256]{1,0:T(8,128)(2,1)S(1)} %get-tuple-element.15), channel_id=1, source_target_pairs={{0,4},{4,0},{8,12},{12,8},{1,5},{5,1},{9,13},{13,9},{2,6},{6,2},{1... | collective-permute-start | bytes 393224 | tf_op jit(solution)/shard_map/ppermute | solution.py:168

commit v3 on v2

--- a/solution.py
+++ b/solution.py
@@ -16,7 +16,7 @@
 LANES = 128
 PERIOD = 64
 ROWS = 32
-CHUNKS = 2
+CHUNKS = 1
 
 
 def phases_of(bit_count):
@@ -45,7 +45,7 @@
 def shift_masks(range_shifts):
     steps = range_shifts + RIM
     bits = [(steps >> k) & 1 for k in range(3)] + [1 - ((steps >> 3) & 1)]
-    return jnp.stack(bits, axis=-1)
+    return jnp.stack(bits, axis=-1).astype(jnp.float32)
 
 
 def merge_kernel(info_ref, taps_ref, masks_ref, weights_ref, table_ref, *refs, places, margin, total, members):
@@ -78,7 +78,7 @@
 
             def rows_step(block, carry, side=side, own=own, level=level, taps=taps, mine=mine):
                 flags = masks_ref[level, mine ^ side, pl.ds(pl.multiple_of(block * ROWS, ROWS), ROWS), :]
-                masks = [jnp.broadcast_to(flags[:, k:k + 1], (ROWS, wide)) != 0 for k in range(4)]
+                masks = [jnp.broadcast_to(flags[:, k:k + 1], (ROWS, wide)).astype(jnp.bfloat16) > 0 for k in range(4)]
                 for p in own:
                     for c in range(2):
                         rows = pl.ds(pl.multiple_of(c * ANGLES + block * ROWS, ROWS), ROWS)
@@ -86,10 +86,12 @@
                         after = pltpu.roll(cells, wide - 1, 1)
                         first = taps[0] * cells + taps[1] * after
                         second = taps[2] * cells + taps[3] * after
-                        v = first + pltpu.roll(second, wide - 2, 1)
+                        v = (first + pltpu.roll(second, wide - 2, 1)).astype(jnp.bfloat16)
                         for k, by in ((0, wide - 1), (1, wide - 2), (2, wide - 4), (3, RIM)):
                             v = jnp.where(masks[k], pltpu.roll(v, by, 1), v)
-                        y_ref[p, rows, :] = v.astype(jnp.bfloat16)
+                        pair = p % 2 ** place + p // 2 ** (place + 1) * 2 ** place
+                        spot = pl.ds(pl.multiple_of((2 * side + c) * ANGLES + block * ROWS, ROWS), ROWS)
+                        y_ref[pair, spot, :] = v
                 return carry
 
             lax.fori_loop(0, ANGLES // ROWS, rows_step, 0)
@@ -100,8 +102,8 @@
             high = low + 2 ** place
             for h in range(2):
                 r0 = h * 2 * ANGLES
-                z = jnp.dot(w_ref[r0:r0 + 2 * ANGLES, 0:2 * ANGLES], y_ref[low], preferred_element_type=jnp.float32)
-                z = z + jnp.dot(w_ref[r0:r0 + 2 * ANGLES, 2 * ANGLES:], y_ref[high], preferred_element_type=jnp.float32)
+                pair = low % 2 ** place + low // 2 ** (place + 1) * 2 ** place
+                z = jnp.dot(w_ref[r0:r0 + 2 * ANGLES, :], y_ref[pair], preferred_element_type=jnp.float32)
                 dest = high if h else low
                 cosine = table_ref[level, 0, mine ^ h]
                 sinus = table_ref[level, 1, mine ^ h]
@@ -118,8 +120,8 @@
                     x_ref[dest, 0:ANGLES, at:at + LANES] = re.astype(jnp.bfloat16)
                     x_ref[dest, ANGLES:, at:at + LANES] = im.astype(jnp.bfloat16)
     for p in range(members):
-        v = x_ref[p].astype(jnp.float32)
-        out_refs[p][...] = pltpu.roll(v, wide - margin, 1)[:, :width].astype(jnp.bfloat16)
+        v = x_ref[p]
+        out_refs[p][...] = pltpu.roll(v, wide - margin, 1)[:, :width]
 
 
 def merge_levels(info, taps, masks, weights, table, pieces, places, margin, total):
@@ -136,7 +138,7 @@
         out_specs=[vmem] * members,
         scratch_shapes=[
             pltpu.VMEM((members, rows, wide), jnp.bfloat16),
-            pltpu.VMEM((members, rows, wide), jnp.bfloat16),
+            pltpu.VMEM((members // 2, 2 * rows, wide), jnp.bfloat16),
             pltpu.VMEM((4 * ANGLES, 4 * ANGLES), jnp.bfloat16),
         ],
         compiler_params=pltpu.CompilerParams(vmem_limit_bytes=32 * 2**20),

time: 106 us -> 90.6 us (0.85)
  waiting for transfers between devices: 12.2 us -> 40.3 us
  Pallas kernels: 41.6 us -> 23.9 us
  starting transfers between devices: 35.4 us -> 18.2 us
  other arithmetic: 9.41 us -> 4.54 us
  local copies, waits for them, and re-layouts: 7.07 us -> 3.33 us
    ppermute x12 -> x6, waiting for transfers between devices: 12.2 us -> 37.5 us  [swap(): return lax.ppermute(value, 'sub', [(i, i ^ mask) for i in range(sub_count)])]
    pallas_call x2 -> x1, Pallas kernels: 41.6 us -> 23.9 us  [merge_levels(): pl.pallas_call(functools.partial(merge_kernel, places=places, margin=marg...]
    ppermute x12 -> x6, starting transfers between devices: 30.4 us -> 14.3 us  [swap(): return lax.ppermute(value, 'sub', [(i, i ^ mask) for i in range(sub_count)])]
    select_n x4 -> x3, other arithmetic: 6.47 us -> 2.77 us  [chosen(): jnp.where(member >> j & 1 == 1, chosen(j - 1, slot ^ 1 << j), chosen(j -...]
    ppermute x1, waiting for transfers between devices: 0.01 us -> 2.7 us  [with_halo(): right = lax.ppermute(head, axis, [(i + 1, i) for i in range(count - 1)])]
    unnamed x15 -> x11, local copies, waits for them, and re-layouts: 3.61 us -> 1.33 us
    another operation x2 -> x1, other arithmetic: 1.61 us -> 0.01 us  [shift_masks(): return jnp.stack(bits, axis=-1).astype(jnp.float32)]
    ppermute x1, starting transfers between devices: 3.69 us -> 2.4 us  [with_halo(): left = lax.ppermute(tail, axis, [(i, i + 1) for i in range(count - 1)])]
  transfers between devices with their start and end apart: 14 -> 8, of which waited for: 3 -> 5; matrix products, arithmetic and copies ran while one was open for 11% -> 3% of each run, Pallas kernels for 39% -> 0%
where the time goes in v3:
time: 90.6 us; the launch traced here: 90.3 us
  waiting for transfers between devices  40.3 us (44%)
  Pallas kernels  23.9 us (26%)
  starting transfers between devices  18.2 us (20%)
  other arithmetic  4.54 us (5%)
  local copies, waits for them, and re-layouts  3.33 us (4%)
    ppermute x6, waiting for transfers between devices, swap(): return lax.ppermute(value, 'sub', [(i, i ^ mask) for i in range(sub_count)])  37.5 us
    pallas_call x1, Pallas kernels, merge_levels(): pl.pallas_call(functools.partial(merge_kernel, places=places, margin=marg...  23.9 us
    ppermute x6, starting transfers between devices, swap(): return lax.ppermute(value, 'sub', [(i, i ^ mask) for i in range(sub_count)])  14.3 us
    select_n x3, other arithmetic, chosen(): jnp.where(member >> j & 1 == 1, chosen(j - 1, slot ^ 1 << j), chosen(j -...  2.77 us
    ppermute x1, waiting for transfers between devices, with_halo(): right = lax.ppermute(head, axis, [(i + 1, i) for i in range(count - 1)])  2.7 us
    ppermute x1, starting transfers between devices, with_halo(): left = lax.ppermute(tail, axis, [(i, i + 1) for i in range(count - 1)])  2.4 us
  transfers between devices with their start and end apart: 8, of which 5 were waited for; matrix products, arithmetic and copies ran while one was open for 3% of the time, Pallas kernels for 0%

profile of v3, /device:TPU:0, one launch (start us, length us, event | category | flops | bytes accessed | tf_op | source)
XLA Modules:
  0.0 90.3 jit_solution(12205727162806907420)
XLA Ops:
  0.0 1.1 %fusion = (bf16[2,2,128,32]{3,2,1,0:T(8,128)(2,1)S(1)}, bf16[2,2,128,32]{3,2,1,0:T(8,128)(2,1)S(1)}) fusion(bf16[2,2,128,1024]{3,2,1,0:T(8,128)(2,1)} %param.5), kind=kLoop, calls=%fused_computation.30 | loop fusion | bytes 131072 | tf_op jit(solution)/shard_map/slice | solution.py:152
  1.1 2.4 %collective-permute-start.1 = (bf16[2,2,128,32]{3,2,1,0:T(8,128)(2,1)S(1)}, bf16[2,2,128,32]{3,2,1,0:T(8,128)(2,1)S(1)}, u32[]{:S(2)}, u32[]{:S(2)}) collective-permute-start(bf16[2,2,128,32]{3,2,1,0:T(8,128)(2,1)S(1)} %get-tuple-element.23), channel_id=1, source_target_pairs={{0,1},{1,2},{2,3},{4,5},{5,6},{6,7},{8,9},{9,10},{10,11},{12,13},{... | collective-permute-start | bytes 98312 | tf_op jit(solution)/shard_map/ppermute | solution.py:153
  3.5 0.0 copy-start.3
  3.5 1.4 %collective-permute-start = (bf16[2,2,128,32]{3,2,1,0:T(8,128)(2,1)S(1)}, bf16[2,2,128,32]{3,2,1,0:T(8,128)(2,1)S(1)}, u32[]{:S(2)}, u32[]{:S(2)}) collective-permute-start(bf16[2,2,128,32]{3,2,1,0:T(8,128)(2,1)S(1)} %get-tuple-element.24), channel_id=1, source_target_pairs={{1,0},{2,1},{3,2},{5,4},{6,5},{7,6},{9,8},{10,9},{11,10},{13,12},{... | collective-permute-start | bytes 98312 | tf_op jit(solution)/shard_map/ppermute | solution.py:154
  4.9 1.3 %constant_dynamic-update-slice_fusion.1 = bf16[2,2,128,1056]{3,2,1,0:T(8,128)(2,1)S(1)} fusion(bf16[2,2,128,1024]{3,2,1,0:T(8,128)(2,1)} %param.5), kind=kLoop, calls=%fused_computation.23 | loop fusion | bytes 2097152
  6.3 2.7 %collective-permute-done = bf16[2,2,128,32]{3,2,1,0:T(8,128)(2,1)S(1)} collective-permute-done((bf16[2,2,128,32]{3,2,1,0:T(8,128)(2,1)S(1)}, bf16[2,2,128,32]{3,2,1,0:T(8,128)(2,1)S(1)}, u32[]{:S(2)}, u32[]{:S(2)}) %collective-permute-start) | collective-permute-done | bytes 32800 | tf_op jit(solution)/shard_map/ppermute | solution.py:154
  9.0 0.0 collective-permute-done.1
  9.0 0.0 copy-done.3
  9.0 1.5 %broadcast_select_fusion.4 = (bf16[2,1,128,576]{3,2,1,0:T(8,128)(2,1)}, bf16[2,1,128,576]{3,2,1,0:T(8,128)(2,1)S(1)}, bf16[2,1,128,576]{3,2,1,0:T(8,128)(2,1)S(1)}) fusion(pred[]{:T(512)S(6)} %eq.4, pred[]{:T(512)S(6)} %eq.5, bf16[2,2,128,1056]{3,2,1,0:T(8,128)(2,1)S(1)} %constant_dynamic-update-slice_fusion, bf16[2,2,128,1024]{3,2,1,0:T(8,128)(2,1)S(1)} %copy-done.3, ...), kind=kLoop, calls=%fused_computation.10 | loop fusion | flops 1622016 | bytes 2555906 | tf_op jit(solution)/shard_map/jit(_where)/select_n | solution.py:162
  10.5 0.0 copy-start.4
  10.5 1.2 %broadcast_select_fusion.5 = (bf16[2,1,128,576]{3,2,1,0:T(8,128)(2,1)}, bf16[2,1,128,576]{3,2,1,0:T(8,128)(2,1)}, bf16[2,1,128,576]{3,2,1,0:T(8,128)(2,1)S(1)}) fusion(pred[]{:T(512)S(6)} %eq.4, bf16[2,1,128,576]{3,2,1,0:T(8,128)(2,1)S(1)} %get-tuple-element.15, bf16[2,1,128,576]{3,2,1,0:T(8,128)(2,1)S(1)} %get-tuple-element.14, pred[]{:T(512)S(6)} %eq.5, ...), kind=kLoop, calls=%fused_computation.11 | loop fusion | flops 1032192 | bytes 2064386 | tf_op jit(solution)/shard_map/jit(_where)/select_n | solution.py:162
  11.7 1.6 %collective-permute-start.2 = (bf16[256,576]{1,0:T(8,128)(2,1)}, bf16[256,576]{1,0:T(8,128)(2,1)S(1)}, u32[]{:S(2)}, u32[]{:S(2)}) collective-permute-start(bf16[256,576]{1,0:T(8,128)(2,1)} %bitcast.7), channel_id=1, source_target_pairs={{0,4},{4,0},{8,12},{12,8},{1,5},{5,1},{9,13},{13,9},{2,6},{6,2},{1... | collective-permute-start | bytes 884744 | tf_op jit(solution)/shard_map/ppermute | solution.py:170
  13.3 2.6 %collective-permute-start.3 = (bf16[256,576]{1,0:T(8,128)(2,1)}, bf16[256,576]{1,0:T(8,128)(2,1)S(1)}, u32[]{:S(2)}, u32[]{:S(2)}) collective-permute-start(bf16[256,576]{1,0:T(8,128)(2,1)} %bitcast.8), channel_id=1, source_target_pairs={{0,8},{4,12},{8,0},{12,4},{1,9},{5,13},{9,1},{13,5},{2,10},{6,14},... | collective-permute-start | bytes 884744 | tf_op jit(solution)/shard_map/ppermute | solution.py:170
  15.9 0.2 collective-permute-start.4
  16.1 0.0 copy-done.4
  16.1 0.2 copy.27
  16.3 0.2 copy.28
  16.6 0.2 copy.29
  16.8 0.2 copy.30
  17.1 0.1 pad_add_fusion.info_ref
  17.1 0.0 copy-start
  17.1 0.0 copy-start.1
  17.1 0.0 copy-start.2
  17.1 0.5 add_convert_fusion.masks_ref
  17.6 7.5 %collective-permute-done.2.refs_1_ = bf16[256,576]{1,0:T(8,128)(2,1)S(1)} collective-permute-done((bf16[256,576]{1,0:T(8,128)(2,1)}, bf16[256,576]{1,0:T(8,128)(2,1)S(1)}, u32[]{:S(2)}, u32[]{:S(2)}) %collective-permute-start.2) | collective-permute-done | bytes 294944 | tf_op jit(solution)/shard_map/ppermute | solution.py:170
  25.1 1.1 %collective-permute-done.3.refs_2_ = bf16[256,576]{1,0:T(8,128)(2,1)S(1)} collective-permute-done((bf16[256,576]{1,0:T(8,128)(2,1)}, bf16[256,576]{1,0:T(8,128)(2,1)S(1)}, u32[]{:S(2)}, u32[]{:S(2)}) %collective-permute-start.3) | collective-permute-done | bytes 294944 | tf_op jit(solution)/shard_map/ppermute | solution.py:170
  26.2 9.9 %collective-permute-done.4.refs_3_ = bf16[256,576]{1,0:T(8,128)(2,1)S(1)} collective-permute-done((bf16[256,576]{1,0:T(8,128)(2,1)}, bf16[256,576]{1,0:T(8,128)(2,1)S(1)}, u32[]{:S(2)}, u32[]{:S(2)}) %collective-permute-start.4) | collective-permute-done | bytes 294944 | tf_op jit(solution)/shard_map/ppermute | solution.py:170
  36.1 0.0 copy-done
  36.1 0.0 copy-done.1
  36.1 0.0 copy-done.2
  36.1 23.9 %merge_levels.1 = (bf16[256,512]{1,0:T(8,128)(2,1)S(1)}, bf16[256,512]{1,0:T(8,128)(2,1)S(1)}, bf16[256,512]{1,0:T(8,128)(2,1)S(1)}, bf16[256,512]{1,0:T(8,128)(2,1)S(1)}) custom-call(s32[2]{0:T(128)S(1)} %pad_add_fusion.info_ref, f32[4,4]{1,0:T(4,128)S(1)} %copy-done.2, f32[4,2,128,4]{3,2,1,0:T(8,128)S(1)} %add_convert_fusion.masks_ref, ...), custom_call_target="tpu_custom_call" | custom-call | tf_op jit(solution)/shard_map/merge_levels/pallas_call | solution.py:134
  60.0 1.4 %collective-permute-start.5 = (bf16[256,512]{1,0:T(8,128)(2,1)S(1)}, bf16[256,512]{1,0:T(8,128)(2,1)S(1)}, u32[]{:S(2)}, u32[]{:S(2)}) collective-permute-start(bf16[256,512]{1,0:T(8,128)(2,1)S(1)} %get-tuple-element.9), channel_id=1, source_target_pairs={{0,12},{4,8},{8,4},{12,0},{1,13},{5,9},{9,5},{13,1},{2,14},{6,10},... | collective-permute-start | bytes 786440 | tf_op jit(solution)/shard_map/ppermute | solution.py:170
  61.4 8.4 %collective-permute-start.6 = (bf16[256,512]{1,0:T(8,128)(2,1)S(1)}, bf16[256,512]{1,0:T(8,128)(2,1)S(1)}, u32[]{:S(2)}, u32[]{:S(2)}) collective-permute-start(bf16[256,512]{1,0:T(8,128)(2,1)S(1)} %get-tuple-element.10), channel_id=1, source_target_pairs={{0,8},{4,12},{8,0},{12,4},{1,9},{5,13},{9,1},{13,5},{2,10},{6,14},... | collective-permute-start | bytes 786440 | tf_op jit(solution)/shard_map/ppermute | solution.py:170
  69.9 0.1 collective-permute-start.7
  70.0 0.0 collective-permute-done.5
  70.0 19.1 %collective-permute-done.6 = bf16[256,512]{1,0:T(8,128)(2,1)S(1)} collective-permute-done((bf16[256,512]{1,0:T(8,128)(2,1)S(1)}, bf16[256,512]{1,0:T(8,128)(2,1)S(1)}, u32[]{:S(2)}, u32[]{:S(2)}) %collective-permute-start.6) | collective-permute-done | bytes 262176 | tf_op jit(solution)/shard_map/ppermute | solution.py:170
  89.0 0.0 collective-permute-done.7
  89.0 0.1 broadcast_select_fusion.15
  89.1 0.1 maximum_bitcast_fusion
  89.3 1.1 %pad_maximum_fusion = bf16[2,2,128,1024]{3,2,1,0:T(8,128)(2,1)} fusion(bf16[2,1,128,1024]{3,2,1,0:T(8,128)(2,1)S(1)} %get-tuple-element.30, bf16[2,1,128,1024]{3,2,1,0:T(8,128)(2,1)S(1)} %get-tuple-element.29), kind=kLoop, calls=%fused_computation | loop fusion | flops 524288 | bytes 2097152 | tf_op jit(solution)/shard_map/stack | solution.py:210
  (2 shorter events, 0.0 us)
Async XLA Ops:
  1.1 7.9 %collective-permute-start.1 = (bf16[2,2,128,32]{3,2,1,0:T(8,128)(2,1)S(1)}, bf16[2,2,128,32]{3,2,1,0:T(8,128)(2,1)S(1)}, u32[]{:S(2)}, u32[]{:S(2)}) collective-permute-start(bf16[2,2,128,32]{3,2,1,0:T(8,128)(2,1)S(1)} %get-tuple-element.23), channel_id=1, source_target_pairs={{0,1},{1,2},{2,3},{4,5},{5,6},{6,7},{8,9},{9,10},{10,11},{12,13},{... | collective-permute-start | bytes 98312 | tf_op jit(solution)/shard_map/ppermute | solution.py:153
  3.5 5.5 %copy-start.3 = (bf16[2,2,128,1024]{3,2,1,0:T(8,128)(2,1)S(1)}, bf16[2,2,128,1024]{3,2,1,0:T(8,128)(2,1)}, u32[]{:S(2)}) copy-start(bf16[2,2,128,1024]{3,2,1,0:T(8,128)(2,1)} %param.5) | copy-start | bytes 3145732
  3.5 5.5 %collective-permute-start = (bf16[2,2,128,32]{3,2,1,0:T(8,128)(2,1)S(1)}, bf16[2,2,128,32]{3,2,1,0:T(8,128)(2,1)S(1)}, u32[]{:S(2)}, u32[]{:S(2)}) collective-permute-start(bf16[2,2,128,32]{3,2,1,0:T(8,128)(2,1)S(1)} %get-tuple-element.24), channel_id=1, source_target_pairs={{1,0},{2,1},{3,2},{5,4},{6,5},{7,6},{9,8},{10,9},{11,10},{13,12},{... | collective-permute-start | bytes 98312 | tf_op jit(solution)/shard_map/ppermute | solution.py:154
  10.5 5.6 %copy-start.4 = (s32[4,2,128]{2,1,0:T(2,128)S(1)}, s32[4,2,128]{2,1,0:T(2,128)}, u32[]{:S(2)}) copy-start(s32[4,2,128]{2,1,0:T(2,128)} %param.8) | copy-start | bytes 12292
  11.7 13.4 %collective-permute-start.2 = (bf16[256,576]{1,0:T(8,128)(2,1)}, bf16[256,576]{1,0:T(8,128)(2,1)S(1)}, u32[]{:S(2)}, u32[]{:S(2)}) collective-permute-start(bf16[256,576]{1,0:T(8,128)(2,1)} %bitcast.7), channel_id=1, source_target_pairs={{0,4},{4,0},{8,12},{12,8},{1,5},{5,1},{9,13},{13,9},{2,6},{6,2},{1... | collective-permute-start | bytes 884744 | tf_op jit(solution)/shard_map/ppermute | solution.py:170
  13.3 12.9 %collective-permute-start.3 = (bf16[256,576]{1,0:T(8,128)(2,1)}, bf16[256,576]{1,0:T(8,128)(2,1)S(1)}, u32[]{:S(2)}, u32[]{:S(2)}) collective-permute-start(bf16[256,576]{1,0:T(8,128)(2,1)} %bitcast.8), channel_id=1, source_target_pairs={{0,8},{4,12},{8,0},{12,4},{1,9},{5,13},{9,1},{13,5},{2,10},{6,14},... | collective-permute-start | bytes 884744 | tf_op jit(solution)/shard_map/ppermute | solution.py:170
  15.9 20.2 %collective-permute-start.4 = (bf16[256,576]{1,0:T(8,128)(2,1)}, bf16[256,576]{1,0:T(8,128)(2,1)S(1)}, u32[]{:S(2)}, u32[]{:S(2)}) collective-permute-start(bf16[256,576]{1,0:T(8,128)(2,1)} %bitcast.9), channel_id=1, source_target_pairs={{0,12},{4,8},{8,4},{12,0},{1,13},{5,9},{9,5},{13,1},{2,14},{6,10},... | collective-permute-start | bytes 884744 | tf_op jit(solution)/shard_map/ppermute | solution.py:170
  17.1 19.0 %copy-start = (bf16[4,2,2,2,128,128]{5,4,3,2,1,0:T(8,128)(2,1)S(1)}, bf16[4,2,2,2,128,128]{5,4,3,2,1,0:T(8,128)(2,1)}, u32[]{:S(2)}) copy-start(bf16[4,2,2,2,128,128]{5,4,3,2,1,0:T(8,128)(2,1)} %weights_ref.1) | copy-start | bytes 3145732
  17.1 19.0 %copy-start.1 = (f32[4,2,2,128,128]{4,3,2,1,0:T(8,128)S(1)}, f32[4,2,2,128,128]{4,3,2,1,0:T(8,128)}, u32[]{:S(2)}) copy-start(f32[4,2,2,128,128]{4,3,2,1,0:T(8,128)} %constant.28.clone.table_ref) | copy-start | bytes 3145732
  17.1 19.0 %copy-start.2 = (f32[4,4]{1,0:T(4,128)S(1)}, f32[4,4]{1,0:T(4,128)}, u32[]{:S(2)}) copy-start(f32[4,4]{1,0:T(4,128)} %taps_ref.1) | copy-start | bytes 196
  60.0 10.0 %collective-permute-start.5 = (bf16[256,512]{1,0:T(8,128)(2,1)S(1)}, bf16[256,512]{1,0:T(8,128)(2,1)S(1)}, u32[]{:S(2)}, u32[]{:S(2)}) collective-permute-start(bf16[256,512]{1,0:T(8,128)(2,1)S(1)} %get-tuple-element.9), channel_id=1, source_target_pairs={{0,12},{4,8},{8,4},{12,0},{1,13},{5,9},{9,5},{13,1},{2,14},{6,10},... | collective-permute-start | bytes 786440 | tf_op jit(solution)/shard_map/ppermute | solution.py:170
  61.4 27.6 %collective-permute-start.6 = (bf16[256,512]{1,0:T(8,128)(2,1)S(1)}, bf16[256,512]{1,0:T(8,128)(2,1)S(1)}, u32[]{:S(2)}, u32[]{:S(2)}) collective-permute-start(bf16[256,512]{1,0:T(8,128)(2,1)S(1)} %get-tuple-element.10), channel_id=1, source_target_pairs={{0,8},{4,12},{8,0},{12,4},{1,9},{5,13},{9,1},{13,5},{2,10},{6,14},... | collective-permute-start | bytes 786440 | tf_op jit(solution)/shard_map/ppermute | solution.py:170
  69.9 19.2 %collective-permute-start.7 = (bf16[256,512]{1,0:T(8,128)(2,1)S(1)}, bf16[256,512]{1,0:T(8,128)(2,1)S(1)}, u32[]{:S(2)}, u32[]{:S(2)}) collective-permute-start(bf16[256,512]{1,0:T(8,128)(2,1)S(1)} %get-tuple-element.11), channel_id=1, source_target_pairs={{0,4},{4,0},{8,12},{12,8},{1,5},{5,1},{9,13},{13,9},{2,6},{6,2},{1... | collective-permute-start | bytes 786440 | tf_op jit(solution)/shard_map/ppermute | solution.py:170

commit v4 on v3

--- a/solution.py
+++ b/solution.py
@@ -16,7 +16,6 @@
 LANES = 128
 PERIOD = 64
 ROWS = 32
-CHUNKS = 1
 
 
 def phases_of(bit_count):
@@ -31,8 +30,8 @@
     return [(levels, bits, sorted(set(bits))) for levels, bits in runs]
 
 
-def phase_table(levels, margin):
-    cols = np.arange(LANES, dtype=np.int64) - margin
+def phase_table(levels):
+    cols = np.arange(LANES, dtype=np.int64)
     rows = np.arange(2 * ANGLES, dtype=np.int64) + 1
     out = []
     for level in levels:
@@ -49,16 +48,21 @@
 
 
 def merge_kernel(info_ref, taps_ref, masks_ref, weights_ref, table_ref, *refs, places, margin, total, members):
-    in_refs, out_refs = refs[:members], refs[members:2 * members]
-    x_ref, y_ref, w_ref = refs[2 * members:]
+    body_refs, strip_refs, out_refs = (refs[i * members:(i + 1) * members] for i in range(3))
+    x_ref, y_ref, w_ref = refs[3 * members:]
     _, _, wide = x_ref.shape
-    given = in_refs[0].shape[-1]
     width = out_refs[0].shape[-1]
     start = info_ref[0]
     n_levels = len(places)
-    x_ref[:, :, wide - LANES:] = jnp.zeros((members, 2 * ANGLES, LANES), jnp.bfloat16)
+    first_part = info_ref[2] == 0
+    gap = jnp.zeros((2 * ANGLES, wide - width - 2 * margin), jnp.float32)
     for q in range(members):
-        x_ref[q, :, 0:given] = in_refs[q][...]
+        x_ref[q, :, 0:width] = body_refs[q][:, 0:width]
+        inner = body_refs[q][:, width:width + margin].astype(jnp.float32)
+        outer = strip_refs[q][...].astype(jnp.float32)
+        right = jnp.where(first_part, inner, outer)
+        left = jnp.where(first_part, outer, inner)
+        x_ref[q, :, width:] = jnp.concatenate([right, gap, left], axis=1).astype(jnp.bfloat16)
     for level in range(n_levels):
         place = places[level]
         mine = (info_ref[1] >> place) & 1
@@ -97,7 +101,8 @@
             lax.fori_loop(0, ANGLES // ROWS, rows_step, 0)
 
         last = level == n_levels - 1
-        cols = start + lax.broadcasted_iota(jnp.int32, (ANGLES, LANES), 1)
+        lane = lax.broadcasted_iota(jnp.int32, (ANGLES, LANES), 1)
+        cols = start + jnp.where(lane < LANES // 2, lane + width, lane - LANES)
         for low in [p for p in range(members) if (p >> place) % 2 == 0]:
             high = low + 2 ** place
             for h in range(2):
@@ -107,34 +112,33 @@
                 dest = high if h else low
                 cosine = table_ref[level, 0, mine ^ h]
                 sinus = table_ref[level, 1, mine ^ h]
-                for tile in range(wide // LANES):
+                for tile in range((width if last else wide) // LANES):
                     at = tile * LANES
                     zr = z[:ANGLES, at:at + LANES]
                     zi = z[ANGLES:, at:at + LANES]
                     re = zr * cosine - zi * sinus
                     im = zr * sinus + zi * cosine
-                    if not last and (at < margin or at + LANES > given - margin):
-                        inside = jnp.logical_and(cols + at >= 0, cols + at < total)
+                    if at == width:
+                        inside = jnp.logical_and(cols >= 0, cols < total)
                         re = jnp.where(inside, re, 0.0)
                         im = jnp.where(inside, im, 0.0)
                     x_ref[dest, 0:ANGLES, at:at + LANES] = re.astype(jnp.bfloat16)
                     x_ref[dest, ANGLES:, at:at + LANES] = im.astype(jnp.bfloat16)
     for p in range(members):
-        v = x_ref[p]
-        out_refs[p][...] = pltpu.roll(v, wide - margin, 1)[:, :width]
-
-
-def merge_levels(info, taps, masks, weights, table, pieces, places, margin, total):
-    members = len(pieces)
-    rows, given = pieces[0].shape
-    width = given - 2 * margin
-    wide = -(-given // LANES) * LANES
+        out_refs[p][...] = x_ref[p, :, 0:width]
+
+
+def merge_levels(info, taps, masks, weights, table, bodies, strips, places, margin, total):
+    members = len(bodies)
+    rows, given = bodies[0].shape
+    width = given - margin
+    wide = width + LANES
     smem = pl.BlockSpec(memory_space=pltpu.SMEM)
     vmem = pl.BlockSpec(memory_space=pltpu.VMEM)
     return pl.pallas_call(
         functools.partial(merge_kernel, places=places, margin=margin, total=total, members=members),
         out_shape=[jax.ShapeDtypeStruct((rows, width), jnp.bfloat16)] * members,
-        in_specs=[smem, smem] + [vmem] * (3 + members),
+        in_specs=[smem, smem] + [vmem] * (3 + 2 * members),
         out_specs=[vmem] * members,
         scratch_shapes=[
             pltpu.VMEM((members, rows, wide), jnp.bfloat16),
@@ -143,16 +147,7 @@
         ],
         compiler_params=pltpu.CompilerParams(vmem_limit_bytes=32 * 2**20),
         name="merge_levels",
-    )(info, taps, masks, weights, table, *pieces)
-
-
-def with_halo(cells, axis, margin):
-    count = lax.axis_size(axis)
-    head = cells[..., :margin]
-    tail = cells[..., cells.shape[-1] - margin:]
-    left = lax.ppermute(tail, axis, [(i, i + 1) for i in range(count - 1)])
-    right = lax.ppermute(head, axis, [(i + 1, i) for i in range(count - 1)])
-    return jnp.concatenate([left, cells, right], axis=-1)
+    )(info, taps, masks, weights, table, *bodies, *strips)
 
 
 def pick(items, q, member):
@@ -168,6 +163,18 @@
         return value
     mask = sum(((q >> j) & 1) << bit for j, bit in enumerate(distinct))
     return lax.ppermute(value, "sub", [(i, i ^ mask) for i in range(sub_count)])
+
+
+def swap_strip(value, q, distinct, groups, sub_count):
+    mask = sum(((q >> j) & 1) << bit for j, bit in enumerate(distinct))
+    count = lax.axis_size("rng")
+    pairs = []
+    for source in range(sub_count):
+        dest = source ^ mask
+        member = sum(((dest >> bit) & 1) << j for j, bit in enumerate(distinct))
+        move = 1 if member // groups == 0 else -1
+        pairs += [(source * count + i, dest * count + i + move) for i in range(count) if 0 <= i + move < count]
+    return lax.ppermute(value, ("sub", "rng"), pairs)
 
 
 def on_device(image, interp_weights, range_taps, range_shifts):
@@ -181,35 +188,31 @@
         members = 2 ** len(distinct)
         parts = members // groups
         width = range_width // parts
-        step = width // CHUNKS
         margin = len(levels) * RIM
+        assert parts == 2 and width % LANES == 0 and 2 * margin < LANES
         first, end = levels[0], levels[-1] + 1
         member = sum(((sub_index >> bit) & 1) << j for j, bit in enumerate(distinct))
-        start = lax.axis_index("rng") * range_width + (member >> (groups.bit_length() - 1)) * width - margin
-        padded = with_halo(current, "rng", margin)
-        table = jnp.asarray(phase_table(levels, margin))
-        columns = [[None] * CHUNKS for _ in range(members)]
-        pieces = []
-        for chunk in range(CHUNKS):
-            windows = []
-            for p in range(members):
-                at = p // groups * width + chunk * step
-                windows.append(padded[:, p % groups, :, at:at + step + 2 * margin])
-            pieces.append([
-                swap(pick(windows, q, member).reshape(2 * ANGLES, step + 2 * margin), q, distinct, sub_count)
-                for q in range(members)
-            ])
-        for chunk in range(CHUNKS):
-            info = jnp.stack([start + chunk * step, member]).astype(jnp.int32)
-            merged = merge_levels(
-                info, range_taps[first:end], masks[first:end], interp_weights[first:end], table,
-                pieces[chunk], [distinct.index(bit) for bit in bits], margin, total)
-            back = [swap(merged[q], q, distinct, sub_count) for q in range(members)]
-            for p in range(members):
-                columns[p][chunk] = pick(back, p, member).reshape(2, ANGLES, step)
+        part = member >> (groups.bit_length() - 1)
+        start = lax.axis_index("rng") * range_width + part * width
+        bodies, strips = [], []
+        for p in range(members):
+            rows = current[:, p % groups].reshape(2 * ANGLES, range_width)
+            if p // groups == 0:
+                bodies.append(rows[:, :width + margin])
+                strips.append(rows[:, range_width - margin:])
+            else:
+                bodies.append(jnp.concatenate([rows[:, width:], rows[:, width - margin:width]], axis=1))
+                strips.append(rows[:, :margin])
+        bodies = [swap(pick(bodies, q, member), q, distinct, sub_count) for q in range(members)]
+        strips = [swap_strip(pick(strips, q, member), q, distinct, groups, sub_count) for q in range(members)]
+        info = jnp.stack([start, member, part]).astype(jnp.int32)
+        merged = merge_levels(
+            info, range_taps[first:end], masks[first:end], interp_weights[first:end], jnp.asarray(phase_table(levels)),
+            bodies, strips, [distinct.index(bit) for bit in bits], margin, total)
+        back = [swap(merged[q], q, distinct, sub_count) for q in range(members)]
+        columns = [pick(back, p, member).reshape(2, ANGLES, width) for p in range(members)]
         current = jnp.stack([
-            jnp.concatenate([columns[part * groups + m][chunk] for part in range(parts) for chunk in range(CHUNKS)], axis=-1)
-            for m in range(groups)
+            jnp.concatenate([columns[k * groups + m] for k in range(parts)], axis=-1) for m in range(groups)
         ], axis=1)
     return current
 

time: 90.6 us -> 96.3 us (1.063)
  starting transfers between devices: 18.2 us -> 21.9 us
  local copies, waits for them, and re-layouts: 3.33 us -> 5.53 us
  waiting for transfers between devices: 40.3 us -> 38.2 us
  other arithmetic: 4.54 us -> 6.31 us
    ppermute x2 -> x4, starting transfers between devices: 3.83 us -> 13.1 us  [swap_strip(): return lax.ppermute(value, ('sub', 'rng'), pairs)]
    ppermute x6, starting transfers between devices: 14.3 us -> 8.84 us  [swap(): return lax.ppermute(value, 'sub', [(i, i ^ mask) for i in range(sub_count)])]
    another operation x4, local copies, waits for them, and re-layouts: 0.9 us -> 4.11 us  [shift_masks(): return jnp.stack(bits, axis=-1).astype(jnp.float32)]
    ppermute x2 -> x4, waiting for transfers between devices: 2.71 us -> 0.8 us  [swap_strip(): return lax.ppermute(value, ('sub', 'rng'), pairs)]
    convert_element_type x1, other arithmetic: 0.47 us -> 2.14 us  [shift_masks(): return jnp.stack(bits, axis=-1).astype(jnp.float32)]
    unnamed x11 -> x8, local copies, waits for them, and re-layouts: 1.33 us -> 0.02 us
    select_n x3 -> x4, other arithmetic: 2.77 us -> 2.89 us  [chosen(): jnp.where(member >> j & 1 == 1, chosen(j - 1, slot ^ 1 << j), chosen(j -...]
  transfers between devices with their start and end apart: 8 -> 10, of which waited for: 5 -> 5; matrix products, arithmetic and copies ran while one was open for 3% -> 9% of each run, Pallas kernels for 0% -> 0%
where the time goes in v4:
time: 96.3 us; the launch traced here: 96.1 us
  waiting for transfers between devices  38.2 us (40%)
  Pallas kernels  24 us (25%)
  starting transfers between devices  21.9 us (23%)
  other arithmetic  6.31 us (7%)
  local copies, waits for them, and re-layouts  5.53 us (6%)
    ppermute x6, waiting for transfers between devices, swap(): return lax.ppermute(value, 'sub', [(i, i ^ mask) for i in range(sub_count)])  37.4 us
    pallas_call x1, Pallas kernels, merge_levels(): pl.pallas_call(functools.partial(merge_kernel, places=places, margin=marg...  24 us
    ppermute x4, starting transfers between devices, swap_strip(): return lax.ppermute(value, ('sub', 'rng'), pairs)  13.1 us
    ppermute x6, starting transfers between devices, swap(): return lax.ppermute(value, 'sub', [(i, i ^ mask) for i in range(sub_count)])  8.84 us
    another operation x4, local copies, waits for them, and re-layouts, shift_masks(): return jnp.stack(bits, axis=-1).astype(jnp.float32)  4.11 us
    select_n x4, other arithmetic, chosen(): jnp.where(member >> j & 1 == 1, chosen(j - 1, slot ^ 1 << j), chosen(j -...  2.89 us
    convert_element_type x1, other arithmetic, shift_masks(): return jnp.stack(bits, axis=-1).astype(jnp.float32)  2.14 us
  transfers between devices with their start and end apart: 10, of which 5 were waited for; matrix products, arithmetic and copies ran while one was open for 9% of the time, Pallas kernels for 0%

profile of v4, /device:TPU:0, one launch (start us, length us, event | category | flops | bytes accessed | tf_op | source)
XLA Modules:
  0.0 96.1 jit_solution(7163269124157653405)
XLA Ops:
  0.0 1.3 %fusion = (bf16[2,1,128,1024]{3,2,1,0:T(8,128)(2,1)S(1)}, bf16[2,1,128,1024]{3,2,1,0:T(8,128)(2,1)S(1)}) fusion(bf16[2,2,128,1024]{3,2,1,0:T(8,128)(2,1)} %param.5), kind=kLoop, calls=%fused_computation.36 | loop fusion | bytes 2097152 | tf_op jit(solution)/shard_map/slice | solution.py:199
  1.3 0.8 broadcast_select_fusion.20
  2.0 0.7 collective-permute-start.6
  2.7 7.5 %collective-permute-start.4 = (bf16[256,32]{1,0:T(8,128)(2,1)}, bf16[256,32]{1,0:T(8,128)(2,1)S(1)}, u32[]{:S(2)}, u32[]{:S(2)}) collective-permute-start(bf16[256,32]{1,0:T(8,128)(2,1)} %get-tuple-element.22), channel_id=1, source_target_pairs={{0,5},{1,6},{2,7},{4,1},{5,2},{6,3},{9,12},{10,13},{11,14},{13,8},... | collective-permute-start | bytes 49160 | tf_op jit(solution)/shard_map/ppermute | solution.py:177
  10.2 0.1 slice.51
  10.3 1.1 %broadcast_select_fusion.4 = (bf16[256,544]{1,0:T(8,128)(2,1)}, bf16[256,544]{1,0:T(8,128)(2,1)}) fusion(pred[]{:T(512)S(6)} %eq.4, bf16[256,1024]{1,0:T(8,128)(2,1)S(1)} %bitcast.24, bf16[256,1024]{1,0:T(8,128)(2,1)S(1)} %bitcast.28, pred[]{:T(512)S(6)} %eq.5, bf16[256,32]{1,0:T(8,128)(2,1)S(1)} %slice.51, bf16[256,512]{1,0:T(8,128)(2,1)S(1)} %slice.50, ...), kind=kLoop, calls=%fused_computation.10 | loop fusion | flops 1671168 | bytes 1671170 | tf_op jit(solution)/shard_map/jit(_where)/select_n | solution.py:157
  11.4 0.1 collective-permute-start.2
  11.6 2.4 %collective-permute-start = (bf16[256,544]{1,0:T(8,128)(2,1)}, bf16[256,544]{1,0:T(8,128)(2,1)}, u32[]{:S(2)}, u32[]{:S(2)}) collective-permute-start(bf16[256,544]{1,0:T(8,128)(2,1)} %get-tuple-element.14), channel_id=1, source_target_pairs={{0,4},{4,0},{8,12},{12,8},{1,5},{5,1},{9,13},{13,9},{2,6},{6,2},{1... | collective-permute-start | bytes 835592 | tf_op jit(solution)/shard_map/ppermute | solution.py:165
  13.9 0.0 copy-start.3
  13.9 0.9 broadcast_select_fusion.5
  14.9 1.9 %collective-permute-start.1 = (bf16[256,544]{1,0:T(8,128)(2,1)}, bf16[256,544]{1,0:T(8,128)(2,1)}, u32[]{:S(2)}, u32[]{:S(2)}) collective-permute-start(bf16[256,544]{1,0:T(8,128)(2,1)} %get-tuple-element.15), channel_id=1, source_target_pairs={{0,8},{4,12},{8,0},{12,4},{1,9},{5,13},{9,1},{13,5},{2,10},{6,14},... | collective-permute-start | bytes 835592 | tf_op jit(solution)/shard_map/ppermute | solution.py:165
  16.8 0.0 copy-done.3
  16.8 1.0 %copy.27 = s32[4,2,128,1]{3,2,1,0:T(8,128)} copy(s32[4,2,128,1]{2,1,0,3:T(2,128)S(1)} %get-tuple-element.28) | data formatting | bytes 8192 | tf_op jit(solution)/shard_map/stack | solution.py:47
  17.8 1.0 %copy.28 = s32[4,2,128,1]{3,2,1,0:T(8,128)} copy(s32[4,2,128,1]{2,1,0,3:T(2,128)S(1)} %get-tuple-element.29) | data formatting | bytes 8192 | tf_op jit(solution)/shard_map/stack | solution.py:47
  18.8 1.0 %copy.29 = s32[4,2,128,1]{3,2,1,0:T(8,128)} copy(s32[4,2,128,1]{2,1,0,3:T(2,128)S(1)} %get-tuple-element.30) | data formatting | bytes 8192 | tf_op jit(solution)/shard_map/stack | solution.py:47
  19.9 1.0 %copy.30 = s32[4,2,128,1]{3,2,1,0:T(8,128)} copy(s32[4,2,128,1]{2,1,0,3:T(2,128)S(1)} %get-tuple-element.31) | data formatting | bytes 8192 | tf_op jit(solution)/shard_map/stack | solution.py:47
  20.9 0.0 copy-start
  20.9 0.0 copy-start.1
  20.9 2.1 %add_convert_fusion.masks_ref = f32[4,2,128,4]{3,2,1,0:T(8,128)S(1)} fusion(s32[4,2,128,1]{3,2,1,0:T(8,128)} %copy.30, s32[4,2,128,1]{3,2,1,0:T(8,128)} %copy.29, s32[4,2,128,1]{3,2,1,0:T(8,128)} %copy.28, s32[4,2,128,1]{3,2,1,0:T(8,128)} %copy.27), kind=kLoop, calls=%fused_computation.1 | loop fusion | flops 16384 | bytes 32768 | tf_op jit(solution)/shard_map/convert_element_type | solution.py:47
  23.1 0.0 collective-permute-done.6.refs_7_
  23.1 0.7 collective-permute-start.5
  23.7 0.0 collective-permute-done.4.refs_5_
  23.8 4.3 %collective-permute-start.3 = (bf16[256,32]{1,0:T(8,128)(2,1)S(1)}, bf16[256,32]{1,0:T(8,128)(2,1)S(1)}, u32[]{:S(2)}, u32[]{:S(2)}) collective-permute-start(bf16[256,32]{1,0:T(8,128)(2,1)S(1)} %get-tuple-element.24), channel_id=1, source_target_pairs={{0,1},{1,2},{2,3},{4,5},{5,6},{6,7},{9,8},{10,9},{11,10},{13,12},{... | collective-permute-start | bytes 49160 | tf_op jit(solution)/shard_map/ppermute | solution.py:177
  28.0 0.0 copy-start.2
  28.1 0.1 pad_add_fusion.info_ref
  28.1 0.0 collective-permute-done.5.refs_6_
  28.1 0.8 collective-permute-done.3.refs_4_
  28.9 0.0 collective-permute-done.2.refs_3_
  28.9 0.9 collective-permute-done.refs_1_
  29.8 16.8 %collective-permute-done.1.refs_2_ = bf16[256,544]{1,0:T(8,128)(2,1)} collective-permute-done((bf16[256,544]{1,0:T(8,128)(2,1)}, bf16[256,544]{1,0:T(8,128)(2,1)}, u32[]{:S(2)}, u32[]{:S(2)}) %collective-permute-start.1) | collective-permute-done | bytes 278560 | tf_op jit(solution)/shard_map/ppermute | solution.py:165
  46.6 0.0 copy-done
  46.6 0.0 copy-done.1
  46.6 0.0 copy-done.2
  46.6 24.0 %merge_levels.1 = (bf16[256,512]{1,0:T(8,128)(2,1)S(1)}, bf16[256,512]{1,0:T(8,128)(2,1)S(1)}, bf16[256,512]{1,0:T(8,128)(2,1)S(1)}, bf16[256,512]{1,0:T(8,128)(2,1)S(1)}) custom-call(s32[3]{0:T(128)S(1)} %pad_add_fusion.info_ref, f32[4,4]{1,0:T(4,128)S(1)} %copy-done.2, f32[4,2,128,4]{3,2,1,0:T(8,128)S(1)} %add_convert_fusion.masks_ref, ...), custom_call_target="tpu_custom_call" | custom-call | tf_op jit(solution)/shard_map/merge_levels/pallas_call | solution.py:138
  70.6 0.2 collective-permute-start.7
  70.8 0.8 collective-permute-start.8
  71.5 3.5 %collective-permute-start.9 = (bf16[256,512]{1,0:T(8,128)(2,1)S(1)}, bf16[256,512]{1,0:T(8,128)(2,1)S(1)}, u32[]{:S(2)}, u32[]{:S(2)}) collective-permute-start(bf16[256,512]{1,0:T(8,128)(2,1)S(1)} %get-tuple-element.11), channel_id=1, source_target_pairs={{0,4},{4,0},{8,12},{12,8},{1,5},{5,1},{9,13},{13,9},{2,6},{6,2},{1... | collective-permute-start | bytes 786440 | tf_op jit(solution)/shard_map/ppermute | solution.py:165
  75.1 6.7 %collective-permute-done.7 = bf16[256,512]{1,0:T(8,128)(2,1)S(1)} collective-permute-done((bf16[256,512]{1,0:T(8,128)(2,1)S(1)}, bf16[256,512]{1,0:T(8,128)(2,1)S(1)}, u32[]{:S(2)}, u32[]{:S(2)}) %collective-permute-start.7) | collective-permute-done | bytes 262176 | tf_op jit(solution)/shard_map/ppermute | solution.py:165
  81.8 13.0 %collective-permute-done.8 = bf16[256,512]{1,0:T(8,128)(2,1)S(1)} collective-permute-done((bf16[256,512]{1,0:T(8,128)(2,1)S(1)}, bf16[256,512]{1,0:T(8,128)(2,1)S(1)}, u32[]{:S(2)}, u32[]{:S(2)}) %collective-permute-start.8) | collective-permute-done | bytes 262176 | tf_op jit(solution)/shard_map/ppermute | solution.py:165
  94.8 0.0 collective-permute-done.9
  94.8 0.1 broadcast_select_fusion.15
  94.9 0.1 maximum_bitcast_fusion
  95.0 1.1 %pad_maximum_fusion = bf16[2,2,128,1024]{3,2,1,0:T(8,128)(2,1)} fusion(bf16[2,1,128,1024]{3,2,1,0:T(8,128)(2,1)S(1)} %get-tuple-element.33, bf16[2,1,128,1024]{3,2,1,0:T(8,128)(2,1)S(1)} %get-tuple-element.32), kind=kLoop, calls=%fused_computation | loop fusion | flops 524288 | bytes 2097152 | tf_op jit(solution)/shard_map/stack | solution.py:214
  (3 shorter events, 0.0 us)
Async XLA Ops:
  2.0 21.0 %collective-permute-start.6 = (bf16[256,32]{1,0:T(8,128)(2,1)}, bf16[256,32]{1,0:T(8,128)(2,1)S(1)}, u32[]{:S(2)}, u32[]{:S(2)}) collective-permute-start(bf16[256,32]{1,0:T(8,128)(2,1)} %get-tuple-element.21), channel_id=1, source_target_pairs={{1,12},{2,13},{3,14},{5,8},{6,9},{7,10},{8,5},{9,6},{10,7},{12,1},... | collective-permute-start | bytes 49160 | tf_op jit(solution)/shard_map/ppermute | solution.py:177
  2.7 21.1 %collective-permute-start.4 = (bf16[256,32]{1,0:T(8,128)(2,1)}, bf16[256,32]{1,0:T(8,128)(2,1)S(1)}, u32[]{:S(2)}, u32[]{:S(2)}) collective-permute-start(bf16[256,32]{1,0:T(8,128)(2,1)} %get-tuple-element.22), channel_id=1, source_target_pairs={{0,5},{1,6},{2,7},{4,1},{5,2},{6,3},{9,12},{10,13},{11,14},{13,8},... | collective-permute-start | bytes 49160 | tf_op jit(solution)/shard_map/ppermute | solution.py:177
  11.4 17.5 %collective-permute-start.2 = (bf16[256,544]{1,0:T(8,128)(2,1)}, bf16[256,544]{1,0:T(8,128)(2,1)S(1)}, u32[]{:S(2)}, u32[]{:S(2)}) collective-permute-start(bf16[256,544]{1,0:T(8,128)(2,1)} %get-tuple-element.13), channel_id=1, source_target_pairs={{0,12},{4,8},{8,4},{12,0},{1,13},{5,9},{9,5},{13,1},{2,14},{6,10},... | collective-permute-start | bytes 835592 | tf_op jit(solution)/shard_map/ppermute | solution.py:165
  11.6 18.2 %collective-permute-start = (bf16[256,544]{1,0:T(8,128)(2,1)}, bf16[256,544]{1,0:T(8,128)(2,1)}, u32[]{:S(2)}, u32[]{:S(2)}) collective-permute-start(bf16[256,544]{1,0:T(8,128)(2,1)} %get-tuple-element.14), channel_id=1, source_target_pairs={{0,4},{4,0},{8,12},{12,8},{1,5},{5,1},{9,13},{13,9},{2,6},{6,2},{1... | collective-permute-start | bytes 835592 | tf_op jit(solution)/shard_map/ppermute | solution.py:165
  13.9 2.9 %copy-start.3 = (s32[4,2,128]{2,1,0:T(2,128)S(1)}, s32[4,2,128]{2,1,0:T(2,128)}, u32[]{:S(2)}) copy-start(s32[4,2,128]{2,1,0:T(2,128)} %param.8) | copy-start | bytes 12292
  14.9 31.7 %collective-permute-start.1 = (bf16[256,544]{1,0:T(8,128)(2,1)}, bf16[256,544]{1,0:T(8,128)(2,1)}, u32[]{:S(2)}, u32[]{:S(2)}) collective-permute-start(bf16[256,544]{1,0:T(8,128)(2,1)} %get-tuple-element.15), channel_id=1, source_target_pairs={{0,8},{4,12},{8,0},{12,4},{1,9},{5,13},{9,1},{13,5},{2,10},{6,14},... | collective-permute-start | bytes 835592 | tf_op jit(solution)/shard_map/ppermute | solution.py:165
  20.9 25.7 %copy-start = (bf16[4,2,2,2,128,128]{5,4,3,2,1,0:T(8,128)(2,1)S(1)}, bf16[4,2,2,2,128,128]{5,4,3,2,1,0:T(8,128)(2,1)}, u32[]{:S(2)}) copy-start(bf16[4,2,2,2,128,128]{5,4,3,2,1,0:T(8,128)(2,1)} %weights_ref.1) | copy-start | bytes 3145732
  20.9 25.7 %copy-start.1 = (f32[4,2,2,128,128]{4,3,2,1,0:T(8,128)S(1)}, f32[4,2,2,128,128]{4,3,2,1,0:T(8,128)}, u32[]{:S(2)}) copy-start(f32[4,2,2,128,128]{4,3,2,1,0:T(8,128)} %constant.25.clone.table_ref) | copy-start | bytes 3145732
  23.1 5.1 %collective-permute-start.5 = (bf16[256,32]{1,0:T(8,128)(2,1)S(1)}, bf16[256,32]{1,0:T(8,128)(2,1)S(1)}, u32[]{:S(2)}, u32[]{:S(2)}) collective-permute-start(bf16[256,32]{1,0:T(8,128)(2,1)S(1)} %get-tuple-element.23), channel_id=1, source_target_pairs={{1,8},{2,9},{3,10},{5,12},{6,13},{7,14},{8,1},{9,2},{10,3},{12,5},... | collective-permute-start | bytes 49160 | tf_op jit(solution)/shard_map/ppermute | solution.py:177
  23.8 5.2 %collective-permute-start.3 = (bf16[256,32]{1,0:T(8,128)(2,1)S(1)}, bf16[256,32]{1,0:T(8,128)(2,1)S(1)}, u32[]{:S(2)}, u32[]{:S(2)}) collective-permute-start(bf16[256,32]{1,0:T(8,128)(2,1)S(1)} %get-tuple-element.24), channel_id=1, source_target_pairs={{0,1},{1,2},{2,3},{4,5},{5,6},{6,7},{9,8},{10,9},{11,10},{13,12},{... | collective-permute-start | bytes 49160 | tf_op jit(solution)/shard_map/ppermute | solution.py:177
  28.0 18.6 %copy-start.2 = (f32[4,4]{1,0:T(4,128)S(1)}, f32[4,4]{1,0:T(4,128)}, u32[]{:S(2)}) copy-start(f32[4,4]{1,0:T(4,128)} %taps_ref.1) | copy-start | bytes 196
  70.6 11.1 %collective-permute-start.7 = (bf16[256,512]{1,0:T(8,128)(2,1)S(1)}, bf16[256,512]{1,0:T(8,128)(2,1)S(1)}, u32[]{:S(2)}, u32[]{:S(2)}) collective-permute-start(bf16[256,512]{1,0:T(8,128)(2,1)S(1)} %get-tuple-element.9), channel_id=1, source_target_pairs={{0,12},{4,8},{8,4},{12,0},{1,13},{5,9},{9,5},{13,1},{2,14},{6,10},... | collective-permute-start | bytes 786440 | tf_op jit(solution)/shard_map/ppermute | solution.py:165
  70.8 24.0 %collective-permute-start.8 = (bf16[256,512]{1,0:T(8,128)(2,1)S(1)}, bf16[256,512]{1,0:T(8,128)(2,1)S(1)}, u32[]{:S(2)}, u32[]{:S(2)}) collective-permute-start(bf16[256,512]{1,0:T(8,128)(2,1)S(1)} %get-tuple-element.10), channel_id=1, source_target_pairs={{0,8},{4,12},{8,0},{12,4},{1,9},{5,13},{9,1},{13,5},{2,10},{6,14},... | collective-permute-start | bytes 786440 | tf_op jit(solution)/shard_map/ppermute | solution.py:165
  71.5 23.3 %collective-permute-start.9 = (bf16[256,512]{1,0:T(8,128)(2,1)S(1)}, bf16[256,512]{1,0:T(8,128)(2,1)S(1)}, u32[]{:S(2)}, u32[]{:S(2)}) collective-permute-start(bf16[256,512]{1,0:T(8,128)(2,1)S(1)} %get-tuple-element.11), channel_id=1, source_target_pairs={{0,4},{4,0},{8,12},{12,8},{1,5},{5,1},{9,13},{13,9},{2,6},{6,2},{1... | collective-permute-start | bytes 786440 | tf_op jit(solution)/shard_map/ppermute | solution.py:165

commit v5 on v4

--- a/solution.py
+++ b/solution.py
@@ -204,7 +204,8 @@
                 bodies.append(jnp.concatenate([rows[:, width:], rows[:, width - margin:width]], axis=1))
                 strips.append(rows[:, :margin])
         bodies = [swap(pick(bodies, q, member), q, distinct, sub_count) for q in range(members)]
-        strips = [swap_strip(pick(strips, q, member), q, distinct, groups, sub_count) for q in range(members)]
+        strips, bodies[1] = lax.optimization_barrier(([pick(strips, q, member) for q in range(members)], bodies[1]))
+        strips = [swap_strip(strips[q], q, distinct, groups, sub_count) for q in range(members)]
         info = jnp.stack([start, member, part]).astype(jnp.int32)
         merged = merge_levels(
             info, range_taps[first:end], masks[first:end], interp_weights[first:end], jnp.asarray(phase_table(levels)),

time: 96.3 us -> 90.2 us (0.937)
  starting transfers between devices: 21.9 us -> 18.5 us
  local copies, waits for them, and re-layouts: 5.53 us -> 2.33 us
  waiting for transfers between devices: 38.2 us -> 40.1 us
  other arithmetic: 6.31 us -> 4.67 us
    ppermute x4, starting transfers between devices: 13.1 us -> 8.16 us  [swap_strip(): return lax.ppermute(value, ('sub', 'rng'), pairs)]
    another operation x4, local copies, waits for them, and re-layouts: 4.11 us -> 0.9 us  [shift_masks(): return jnp.stack(bits, axis=-1).astype(jnp.float32)]
    ppermute x6, waiting for transfers between devices: 37.4 us -> 40.1 us  [swap(): return lax.ppermute(value, 'sub', [(i, i ^ mask) for i in range(sub_count)])]
    convert_element_type x1, other arithmetic: 2.14 us -> 0.47 us  [shift_masks(): return jnp.stack(bits, axis=-1).astype(jnp.float32)]
    ppermute x6, starting transfers between devices: 8.84 us -> 10.3 us  [swap(): return lax.ppermute(value, 'sub', [(i, i ^ mask) for i in range(sub_count)])]
  transfers between devices with their start and end apart: 10 -> 10, of which waited for: 5 -> 4; matrix products, arithmetic and copies ran while one was open for 9% -> 3% of each run, Pallas kernels for 0% -> 0%
where the time goes in v5:
time: 90.2 us; the launch traced here: 89.4 us
  waiting for transfers between devices  40.1 us (44%)
  Pallas kernels  23.6 us (26%)
  starting transfers between devices  18.5 us (21%)
  other arithmetic  4.67 us (5%)
  local copies, waits for them, and re-layouts  2.33 us (3%)
    ppermute x6, waiting for transfers between devices, swap(): return lax.ppermute(value, 'sub', [(i, i ^ mask) for i in range(sub_count)])  40.1 us
    pallas_call x1, Pallas kernels, merge_levels(): pl.pallas_call(functools.partial(merge_kernel, places=places, margin=marg...  23.6 us
    ppermute x6, starting transfers between devices, swap(): return lax.ppermute(value, 'sub', [(i, i ^ mask) for i in range(sub_count)])  10.3 us
    ppermute x4, starting transfers between devices, swap_strip(): return lax.ppermute(value, ('sub', 'rng'), pairs)  8.16 us
    select_n x4, other arithmetic, chosen(): jnp.where(member >> j & 1 == 1, chosen(j - 1, slot ^ 1 << j), chosen(j -...  2.9 us
  transfers between devices with their start and end apart: 10, of which 4 were waited for; matrix products, arithmetic and copies ran while one was open for 3% of the time, Pallas kernels for 0%

profile of v5, /device:TPU:0, one launch (start us, length us, event | category | flops | bytes accessed | tf_op | source)
XLA Modules:
  0.0 89.4 jit_solution(1139574564190787556)
XLA Ops:
  0.0 1.3 %fusion = (bf16[2,1,128,1024]{3,2,1,0:T(8,128)(2,1)S(1)}, bf16[2,1,128,1024]{3,2,1,0:T(8,128)(2,1)S(1)}) fusion(bf16[2,2,128,1024]{3,2,1,0:T(8,128)(2,1)} %param.5), kind=kLoop, calls=%fused_computation.36 | loop fusion | bytes 2097152 | tf_op jit(solution)/shard_map/slice | solution.py:199
  1.3 0.1 slice.51
  1.4 0.8 broadcast_select_fusion.20
  2.2 1.1 %broadcast_select_fusion.4 = (bf16[256,544]{1,0:T(8,128)(2,1)}, bf16[256,544]{1,0:T(8,128)(2,1)}) fusion(pred[]{:T(512)S(6)} %eq.4, bf16[256,1024]{1,0:T(8,128)(2,1)S(1)} %bitcast.24, bf16[256,1024]{1,0:T(8,128)(2,1)S(1)} %bitcast.28, pred[]{:T(512)S(6)} %eq.5, bf16[256,32]{1,0:T(8,128)(2,1)S(1)} %slice.51, bf16[256,512]{1,0:T(8,128)(2,1)S(1)} %slice.50, ...), kind=kLoop, calls=%fused_computation.10 | loop fusion | flops 1671168 | bytes 1671170 | tf_op jit(solution)/shard_map/jit(_where)/select_n | solution.py:157
  3.3 5.1 %collective-permute-start.2 = (bf16[256,544]{1,0:T(8,128)(2,1)}, bf16[256,544]{1,0:T(8,128)(2,1)S(1)}, u32[]{:S(2)}, u32[]{:S(2)}) collective-permute-start(bf16[256,544]{1,0:T(8,128)(2,1)} %get-tuple-element.23), channel_id=1, source_target_pairs={{0,12},{4,8},{8,4},{12,0},{1,13},{5,9},{9,5},{13,1},{2,14},{6,10},... | collective-permute-start | bytes 835592 | tf_op jit(solution)/shard_map/ppermute | solution.py:165
  8.4 0.0 collective-permute-start
  8.4 0.0 copy-start.5
  8.4 0.9 %broadcast_select_fusion.5 = (bf16[256,544]{1,0:T(8,128)(2,1)}, bf16[256,544]{1,0:T(8,128)(2,1)S(1)}) fusion(pred[]{:T(512)S(6)} %eq.4, bf16[256,1024]{1,0:T(8,128)(2,1)S(1)} %bitcast.29, bf16[256,1024]{1,0:T(8,128)(2,1)S(1)} %bitcast.25, pred[]{:T(512)S(6)} %eq.5, bf16[256,32]{1,0:T(8,128)(2,1)S(1)} %get-tuple-element.37, bf16[256,512]{1,0:T(8,128)(2,1)S(1)} %slice.52, ...), kind=kLoop, calls=%fused_computation.11 | loop fusion | flops 1671168 | bytes 1671170 | tf_op jit(solution)/shard_map/jit(_where)/select_n | solution.py:157
  9.3 0.6 collective-permute-start.1
  9.9 0.0 copy-done.5
  9.9 0.2 copy.27
  10.1 0.2 copy.28
  10.4 0.2 copy.29
  10.6 0.2 copy.30
  10.8 0.0 copy-start.4
  10.9 0.0 copy-start.3
  10.9 0.0 copy-start
  10.9 0.0 copy-start.1
  10.9 0.5 add_convert_fusion.masks_ref
  11.4 13.0 %collective-permute-done.refs_1_ = bf16[256,544]{1,0:T(8,128)(2,1)S(1)} collective-permute-done((bf16[256,544]{1,0:T(8,128)(2,1)}, bf16[256,544]{1,0:T(8,128)(2,1)S(1)}, u32[]{:S(2)}, u32[]{:S(2)}) %collective-permute-start) | collective-permute-done | bytes 278560 | tf_op jit(solution)/shard_map/ppermute | solution.py:165
  24.4 0.0 copy-done.4
  24.4 1.9 %collective-permute-start.3 = (bf16[256,32]{1,0:T(8,128)(2,1)S(1)}, bf16[256,32]{1,0:T(8,128)(2,1)S(1)}, u32[]{:S(2)}, u32[]{:S(2)}) collective-permute-start(bf16[256,32]{1,0:T(8,128)(2,1)S(1)} %copy-done.4), channel_id=1, source_target_pairs={{0,1},{1,2},{2,3},{4,5},{5,6},{6,7},{9,8},{10,9},{11,10},{13,12},{... | collective-permute-start | bytes 49160 | tf_op jit(solution)/shard_map/ppermute | solution.py:177
  26.3 0.0 copy-done.3
  26.3 4.9 %collective-permute-start.4 = (bf16[256,32]{1,0:T(8,128)(2,1)S(1)}, bf16[256,32]{1,0:T(8,128)(2,1)S(1)}, u32[]{:S(2)}, u32[]{:S(2)}) collective-permute-start(bf16[256,32]{1,0:T(8,128)(2,1)S(1)} %copy-done.3), channel_id=1, source_target_pairs={{0,5},{1,6},{2,7},{4,1},{5,2},{6,3},{9,12},{10,13},{11,14},{13,8},... | collective-permute-start | bytes 49160 | tf_op jit(solution)/shard_map/ppermute | solution.py:177
  31.2 0.7 collective-permute-start.5
  31.9 0.0 collective-permute-done.2.refs_3_
  31.9 0.7 collective-permute-start.6
  32.6 0.0 copy-start.2
  32.6 0.1 pad_add_fusion.info_ref
  32.7 6.2 %collective-permute-done.1.refs_2_ = bf16[256,544]{1,0:T(8,128)(2,1)S(1)} collective-permute-done((bf16[256,544]{1,0:T(8,128)(2,1)}, bf16[256,544]{1,0:T(8,128)(2,1)S(1)}, u32[]{:S(2)}, u32[]{:S(2)}) %collective-permute-start.1) | collective-permute-done | bytes 278560 | tf_op jit(solution)/shard_map/ppermute | solution.py:165
  38.9 0.0 collective-permute-done.3.refs_4_
  38.9 0.0 collective-permute-done.4.refs_5_
  38.9 0.0 collective-permute-done.5.refs_6_
  38.9 0.0 collective-permute-done.6.refs_7_
  38.9 0.0 copy-done
  38.9 0.0 copy-done.1
  38.9 0.0 copy-done.2
  39.0 23.6 %merge_levels.1 = (bf16[256,512]{1,0:T(8,128)(2,1)S(1)}, bf16[256,512]{1,0:T(8,128)(2,1)S(1)}, bf16[256,512]{1,0:T(8,128)(2,1)S(1)}, bf16[256,512]{1,0:T(8,128)(2,1)S(1)}) custom-call(s32[3]{0:T(128)S(1)} %pad_add_fusion.info_ref, f32[4,4]{1,0:T(4,128)S(1)} %copy-done.2, f32[4,2,128,4]{3,2,1,0:T(8,128)S(1)} %add_convert_fusion.masks_ref, ...), custom_call_target="tpu_custom_call" | custom-call | tf_op jit(solution)/shard_map/merge_levels/pallas_call | solution.py:138
  62.6 4.0 %collective-permute-start.7 = (bf16[256,512]{1,0:T(8,128)(2,1)S(1)}, bf16[256,512]{1,0:T(8,128)(2,1)S(1)}, u32[]{:S(2)}, u32[]{:S(2)}) collective-permute-start(bf16[256,512]{1,0:T(8,128)(2,1)S(1)} %get-tuple-element.19), channel_id=1, source_target_pairs={{0,12},{4,8},{8,4},{12,0},{1,13},{5,9},{9,5},{13,1},{2,14},{6,10},... | collective-permute-start | bytes 786440 | tf_op jit(solution)/shard_map/ppermute | solution.py:165
  66.6 0.0 collective-permute-start.8
  66.6 0.6 collective-permute-start.9
  67.2 5.5 %collective-permute-done.7 = bf16[256,512]{1,0:T(8,128)(2,1)S(1)} collective-permute-done((bf16[256,512]{1,0:T(8,128)(2,1)S(1)}, bf16[256,512]{1,0:T(8,128)(2,1)S(1)}, u32[]{:S(2)}, u32[]{:S(2)}) %collective-permute-start.7) | collective-permute-done | bytes 262176 | tf_op jit(solution)/shard_map/ppermute | solution.py:165
  72.8 15.3 %collective-permute-done.8 = bf16[256,512]{1,0:T(8,128)(2,1)S(1)} collective-permute-done((bf16[256,512]{1,0:T(8,128)(2,1)S(1)}, bf16[256,512]{1,0:T(8,128)(2,1)S(1)}, u32[]{:S(2)}, u32[]{:S(2)}) %collective-permute-start.8) | collective-permute-done | bytes 262176 | tf_op jit(solution)/shard_map/ppermute | solution.py:165
  88.1 0.0 collective-permute-done.9
  88.1 0.1 broadcast_select_fusion.15
  88.2 0.1 maximum_bitcast_fusion
  88.3 1.1 %pad_maximum_fusion = bf16[2,2,128,1024]{3,2,1,0:T(8,128)(2,1)} fusion(bf16[2,1,128,1024]{3,2,1,0:T(8,128)(2,1)S(1)} %get-tuple-element.43, bf16[2,1,128,1024]{3,2,1,0:T(8,128)(2,1)S(1)} %get-tuple-element.42), kind=kLoop, calls=%fused_computation | loop fusion | flops 524288 | bytes 2097152 | tf_op jit(solution)/shard_map/stack | solution.py:215
  (3 shorter events, 0.0 us)
Async XLA Ops:
  3.3 28.6 %collective-permute-start.2 = (bf16[256,544]{1,0:T(8,128)(2,1)}, bf16[256,544]{1,0:T(8,128)(2,1)S(1)}, u32[]{:S(2)}, u32[]{:S(2)}) collective-permute-start(bf16[256,544]{1,0:T(8,128)(2,1)} %get-tuple-element.23), channel_id=1, source_target_pairs={{0,12},{4,8},{8,4},{12,0},{1,13},{5,9},{9,5},{13,1},{2,14},{6,10},... | collective-permute-start | bytes 835592 | tf_op jit(solution)/shard_map/ppermute | solution.py:165
  8.4 16.0 %collective-permute-start = (bf16[256,544]{1,0:T(8,128)(2,1)}, bf16[256,544]{1,0:T(8,128)(2,1)S(1)}, u32[]{:S(2)}, u32[]{:S(2)}) collective-permute-start(bf16[256,544]{1,0:T(8,128)(2,1)} %get-tuple-element.24), channel_id=1, source_target_pairs={{0,4},{4,0},{8,12},{12,8},{1,5},{5,1},{9,13},{13,9},{2,6},{6,2},{1... | collective-permute-start | bytes 835592 | tf_op jit(solution)/shard_map/ppermute | solution.py:165
  8.4 1.5 %copy-start.5 = (s32[4,2,128]{2,1,0:T(2,128)S(1)}, s32[4,2,128]{2,1,0:T(2,128)}, u32[]{:S(2)}) copy-start(s32[4,2,128]{2,1,0:T(2,128)} %param.8) | copy-start | bytes 12292
  9.3 29.6 %collective-permute-start.1 = (bf16[256,544]{1,0:T(8,128)(2,1)}, bf16[256,544]{1,0:T(8,128)(2,1)S(1)}, u32[]{:S(2)}, u32[]{:S(2)}) collective-permute-start(bf16[256,544]{1,0:T(8,128)(2,1)} %get-tuple-element.25), channel_id=1, source_target_pairs={{0,8},{4,12},{8,0},{12,4},{1,9},{5,13},{9,1},{13,5},{2,10},{6,14},... | collective-permute-start | bytes 835592 | tf_op jit(solution)/shard_map/ppermute | solution.py:165
  10.8 13.5 %copy-start.4 = (bf16[256,32]{1,0:T(8,128)(2,1)S(1)}, bf16[256,32]{1,0:T(8,128)(2,1)}, u32[]{:S(2)}) copy-start(bf16[256,32]{1,0:T(8,128)(2,1)} %get-tuple-element.15) | copy-start | bytes 49156
  10.9 15.4 %copy-start.3 = (bf16[256,32]{1,0:T(8,128)(2,1)S(1)}, bf16[256,32]{1,0:T(8,128)(2,1)}, u32[]{:S(2)}) copy-start(bf16[256,32]{1,0:T(8,128)(2,1)} %get-tuple-element.16) | copy-start | bytes 49156
  10.9 28.1 %copy-start = (bf16[4,2,2,2,128,128]{5,4,3,2,1,0:T(8,128)(2,1)S(1)}, bf16[4,2,2,2,128,128]{5,4,3,2,1,0:T(8,128)(2,1)}, u32[]{:S(2)}) copy-start(bf16[4,2,2,2,128,128]{5,4,3,2,1,0:T(8,128)(2,1)} %weights_ref.1) | copy-start | bytes 3145732
  10.9 28.1 %copy-start.1 = (f32[4,2,2,128,128]{4,3,2,1,0:T(8,128)S(1)}, f32[4,2,2,128,128]{4,3,2,1,0:T(8,128)}, u32[]{:S(2)}) copy-start(f32[4,2,2,128,128]{4,3,2,1,0:T(8,128)} %constant.25.clone.table_ref) | copy-start | bytes 3145732
  24.4 14.5 %collective-permute-start.3 = (bf16[256,32]{1,0:T(8,128)(2,1)S(1)}, bf16[256,32]{1,0:T(8,128)(2,1)S(1)}, u32[]{:S(2)}, u32[]{:S(2)}) collective-permute-start(bf16[256,32]{1,0:T(8,128)(2,1)S(1)} %copy-done.4), channel_id=1, source_target_pairs={{0,1},{1,2},{2,3},{4,5},{5,6},{6,7},{9,8},{10,9},{11,10},{13,12},{... | collective-permute-start | bytes 49160 | tf_op jit(solution)/shard_map/ppermute | solution.py:177
  26.3 12.6 %collective-permute-start.4 = (bf16[256,32]{1,0:T(8,128)(2,1)S(1)}, bf16[256,32]{1,0:T(8,128)(2,1)S(1)}, u32[]{:S(2)}, u32[]{:S(2)}) collective-permute-start(bf16[256,32]{1,0:T(8,128)(2,1)S(1)} %copy-done.3), channel_id=1, source_target_pairs={{0,5},{1,6},{2,7},{4,1},{5,2},{6,3},{9,12},{10,13},{11,14},{13,8},... | collective-permute-start | bytes 49160 | tf_op jit(solution)/shard_map/ppermute | solution.py:177
  31.2 7.7 %collective-permute-start.5 = (bf16[256,32]{1,0:T(8,128)(2,1)S(1)}, bf16[256,32]{1,0:T(8,128)(2,1)S(1)}, u32[]{:S(2)}, u32[]{:S(2)}) collective-permute-start(bf16[256,32]{1,0:T(8,128)(2,1)S(1)} %get-tuple-element.17), channel_id=1, source_target_pairs={{1,8},{2,9},{3,10},{5,12},{6,13},{7,14},{8,1},{9,2},{10,3},{12,5},... | collective-permute-start | bytes 49160 | tf_op jit(solution)/shard_map/ppermute | solution.py:177
  31.9 7.0 %collective-permute-start.6 = (bf16[256,32]{1,0:T(8,128)(2,1)S(1)}, bf16[256,32]{1,0:T(8,128)(2,1)S(1)}, u32[]{:S(2)}, u32[]{:S(2)}) collective-permute-start(bf16[256,32]{1,0:T(8,128)(2,1)S(1)} %get-tuple-element.18), channel_id=1, source_target_pairs={{1,12},{2,13},{3,14},{5,8},{6,9},{7,10},{8,5},{9,6},{10,7},{12,1},... | collective-permute-start | bytes 49160 | tf_op jit(solution)/shard_map/ppermute | solution.py:177
  32.6 6.4 %copy-start.2 = (f32[4,4]{1,0:T(4,128)S(1)}, f32[4,4]{1,0:T(4,128)}, u32[]{:S(2)}) copy-start(f32[4,4]{1,0:T(4,128)} %taps_ref.1) | copy-start | bytes 196
  62.6 10.2 %collective-permute-start.7 = (bf16[256,512]{1,0:T(8,128)(2,1)S(1)}, bf16[256,512]{1,0:T(8,128)(2,1)S(1)}, u32[]{:S(2)}, u32[]{:S(2)}) collective-permute-start(bf16[256,512]{1,0:T(8,128)(2,1)S(1)} %get-tuple-element.19), channel_id=1, source_target_pairs={{0,12},{4,8},{8,4},{12,0},{1,13},{5,9},{9,5},{13,1},{2,14},{6,10},... | collective-permute-start | bytes 786440 | tf_op jit(solution)/shard_map/ppermute | solution.py:165
  66.6 21.5 %collective-permute-start.8 = (bf16[256,512]{1,0:T(8,128)(2,1)S(1)}, bf16[256,512]{1,0:T(8,128)(2,1)S(1)}, u32[]{:S(2)}, u32[]{:S(2)}) collective-permute-start(bf16[256,512]{1,0:T(8,128)(2,1)S(1)} %get-tuple-element.20), channel_id=1, source_target_pairs={{0,8},{4,12},{8,0},{12,4},{1,9},{5,13},{9,1},{13,5},{2,10},{6,14},... | collective-permute-start | bytes 786440 | tf_op jit(solution)/shard_map/ppermute | solution.py:165
  66.6 21.5 %collective-permute-start.9 = (bf16[256,512]{1,0:T(8,128)(2,1)S(1)}, bf16[256,512]{1,0:T(8,128)(2,1)S(1)}, u32[]{:S(2)}, u32[]{:S(2)}) collective-permute-start(bf16[256,512]{1,0:T(8,128)(2,1)S(1)} %get-tuple-element.21), channel_id=1, source_target_pairs={{0,4},{4,0},{8,12},{12,8},{1,5},{5,1},{9,13},{13,9},{2,6},{6,2},{1... | collective-permute-start | bytes 786440 | tf_op jit(solution)/shard_map/ppermute | solution.py:165
